TPU v7x, 32 devices: a whole 2x2x4 slice. The times are simulated.
32 devices in a mesh: dp: 8 (over z, x), ctx: 4 (over y, core).
Axes of the slice: x: 2, y: 2, z: 4, core: 2. Of those that a mesh axis runs over, the one named last changes fastest.
Arguments:
- stream: bfloat16 [8, 512, 4096], P('dp', 'ctx'), may hold values from -6 to 6
- queries: bfloat16 [8, 512, 2048], P('dp', 'ctx'), may hold values from -150 to 150
- keys: bfloat16 [8, 512, 512], P('dp', 'ctx'), may hold values from -6 to 6
- values: bfloat16 [8, 512, 512], P('dp', 'ctx'), may hold values from -6 to 6
- clip_lengths: int32 [8], P('dp'), may hold values from 256 to 512, as said below
- mod_shift: float32 [8, 4096], P('dp'), may hold values from -3 to 3
- mod_scale: float32 [8, 4096], P('dp'), may hold values from -0.5 to 0.5
- out_weight: bfloat16 [2048, 4096], P('ctx', 'dp'), may hold values from -2 to 2
- final_weight: bfloat16 [4096, 128], replicated, may hold values from -0.09375 to 0.09375
- noisy_latents: bfloat16 [8, 512, 128], P('dp', 'ctx'), may hold values from -6 to 6
- timestep: int32 [8], P('dp'), may hold values from 100 to 599
- crop_map: int32 [8, 256], P('dp'), may hold values from 0 to 511, as said below
- embed_weight: bfloat16 [128, 1408], replicated, may hold values from -0.5 to 0.5
- pre_gain: float32 [1408], replicated, may hold values from 0.1 to 1.9
- up_weight: bfloat16 [1408, 6144], P(None, 'ctx'), may hold values from -0.15625 to 0.15625
- down_weight: bfloat16 [6144, 1408], P('ctx'), may hold values from -0.21875 to 0.21875
- post_gain: float32 [1408], replicated, may hold values from 0.1 to 1.9
- head_weight: float32 [1408], replicated, may hold values from -4 to 4
Outputs:
- reward: float32 [8], P('dp')
- grad_stream: bfloat16 [8, 512, 4096], P('dp', 'ctx')
- grad_queries: bfloat16 [8, 512, 2048], P('dp', 'ctx')
Inputs may be any that keep to these rules, and one draw needn't show every extreme that they name: `clip_lengths`: each clip's length lies between 256 and 512; in every draw some clip has length exactly 512. `crop_map`: every crop token of clip b points below clip_lengths[b].
All inputs are finite; a program needn't handle non-finite values.
Results may differ from a plain program's by a relative error of at most 0.04.
Values may be sent and summed in bfloat16 or wider, within the bound.
A program may use at most 128 MiB of HBM per device.

v0:
```python
import math

import jax
import jax.numpy as jnp
from jax import lax
from jax.sharding import PartitionSpec as P

HEADS = 16
KV_HEADS = 4
HEAD = 128
PATCH = 128


MASKED = -1e30
LOSS_SCALE = 16.0
EPSILON = 1e-06


def plan(noise_step):
    phase = (noise_step.astype(jnp.float32) / 1000.0 + 0.008) / 1.008 * (math.pi / 2.0)
    signal_root = jnp.cos(phase)
    return (signal_root, jnp.sqrt(1.0 - signal_root * signal_root))


def gelu_slope(hidden, upstream):
    return jax.vjp(lambda argument: jax.nn.gelu(argument, approximate=True), hidden)[1](upstream)[0]


def keep_state(current):
    return current


def per_device(
    stream,
    queries,
    keys,
    values,
    clip_lengths,
    mod_shift,
    mod_scale,
    out_weight,
    final_weight,
    noisy_latents,
    timestep,
    crop_map,
    embed_weight,
    pre_gain,
    up_weight,
    down_weight,
    post_gain,
    head_weight,
):
    tokens = queries.shape[1]
    per_group = HEADS // KV_HEADS
    clip_length = clip_lengths[0]
    query_heads = queries[0].reshape(tokens, KV_HEADS, per_group, HEAD)

    def key_scores(key_piece):
        row_count = key_piece.shape[0]
        scores = jnp.einsum(
            "tkgd,skd->kgts",
            query_heads,
            key_piece.reshape(row_count, KV_HEADS, HEAD),
            preferred_element_type=jnp.float32,
        ) / math.sqrt(HEAD)
        is_live = jnp.arange(row_count, dtype=jnp.int32) < clip_length
        return jnp.where(is_live, scores, MASKED)

    shape_heads = (KV_HEADS, per_group, tokens)
    start_state = (
        jnp.full(shape_heads, -jnp.inf, jnp.float32),
        jnp.zeros(shape_heads, jnp.float32),
        jnp.zeros(shape_heads + (HEAD,), jnp.float32),
    )
    key_piece = lax.all_gather(keys[0], "ctx", axis=0, tiled=True)
    value_piece = lax.all_gather(values[0], "ctx", axis=0, tiled=True)

    def forward_advance(current):
        highest, denominator, numerator = current
        row_count = key_piece.shape[0]
        scores = key_scores(key_piece)
        new_highest = jnp.max(scores, axis=-1)
        factor = jnp.exp(highest - new_highest)
        weights_rows = jnp.exp(scores - new_highest[..., None])
        blended = jnp.einsum(
            "kgts,skd->kgtd",
            weights_rows.astype(jnp.bfloat16),
            value_piece.reshape(row_count, KV_HEADS, HEAD),
            preferred_element_type=jnp.float32,
        )
        return (
            new_highest,
            denominator * factor + jnp.sum(weights_rows, axis=-1),
            numerator * factor[..., None] + blended,
        )

    highest, denominator, numerator = lax.cond(
        jnp.int32(0) < clip_length, forward_advance, keep_state, start_state
    )
    attended = (
        jnp.transpose(numerator / denominator[..., None], (2, 0, 1, 3))
        .reshape(tokens, HEADS * HEAD)
        .astype(jnp.bfloat16)
    )
    log_total = highest + jnp.log(denominator)
    column_full = lax.all_gather(out_weight, "dp", axis=1, tiled=True)
    full_weight = lax.all_gather(column_full, "ctx", axis=0, tiled=True)
    residual = stream[0].astype(jnp.float32) + jnp.dot(
        attended, full_weight, preferred_element_type=jnp.float32
    )
    centred = residual - jnp.mean(residual, axis=-1, keepdims=True)
    inverse = lax.rsqrt(jnp.mean(centred * centred, axis=-1, keepdims=True) + EPSILON)
    unit_rows = centred * inverse
    gain_rows = 1.0 + mod_scale[0]
    modulated = (unit_rows * gain_rows + mod_shift[0]).astype(jnp.bfloat16)
    predicted = jnp.dot(modulated, final_weight, preferred_element_type=jnp.float32)
    signal_root, noise_root = plan(timestep[0])
    denoised = (
        (noisy_latents[0].astype(jnp.float32) - noise_root * predicted) / signal_root
    ).astype(jnp.bfloat16)
    gathered = lax.all_gather(denoised, "ctx", axis=0, tiled=True)
    crop_rows = crop_map[0]
    crop_tokens = jnp.take(gathered, crop_rows, axis=0)
    embedded = jnp.dot(crop_tokens, embed_weight, preferred_element_type=jnp.float32)
    first_root = jnp.sqrt(jnp.mean(embedded * embedded, axis=-1, keepdims=True) + EPSILON)
    first_unit = embedded / first_root
    normed = (first_unit * pre_gain).astype(jnp.bfloat16)
    hidden = jnp.dot(normed, up_weight, preferred_element_type=jnp.float32)
    active = jax.nn.gelu(hidden, approximate=True).astype(jnp.bfloat16)
    row_total = embedded.shape[0]
    head_slope = -(LOSS_SCALE / row_total) * head_weight * post_gain
    summed = embedded + lax.psum(
        jnp.dot(active, down_weight, preferred_element_type=jnp.float32).astype(jnp.bfloat16), "ctx"
    ).astype(jnp.float32)
    second_root = jnp.sqrt(jnp.mean(summed * summed, axis=-1, keepdims=True) + EPSILON)
    second_unit = summed / second_root
    reward = jnp.mean(jnp.sum(second_unit * post_gain * head_weight, axis=-1))
    summed_slope = (
        head_slope - second_unit * jnp.mean(head_slope * second_unit, axis=-1, keepdims=True)
    ) / second_root
    active_slope = jnp.einsum(
        "rw,hw->rh",
        summed_slope.astype(jnp.bfloat16),
        down_weight,
        preferred_element_type=jnp.float32,
    )
    hidden_slope = gelu_slope(hidden, active_slope).astype(jnp.bfloat16)
    normed_slope = (
        lax.psum(
            jnp.einsum(
                "rh,wh->rw", hidden_slope, up_weight, preferred_element_type=jnp.float32
            ).astype(jnp.bfloat16),
            "ctx",
        ).astype(jnp.float32)
        * pre_gain
    )
    embed_slope = (
        summed_slope
        + (normed_slope - first_unit * jnp.mean(normed_slope * first_unit, axis=-1, keepdims=True))
        / first_root
    )
    token_slope = jnp.einsum(
        "rw,pw->rp",
        embed_slope.astype(jnp.bfloat16),
        embed_weight,
        preferred_element_type=jnp.float32,
    )
    latent_full = jnp.zeros((gathered.shape[0], PATCH), jnp.float32).at[crop_rows].add(token_slope)
    latent_slope = lax.dynamic_slice_in_dim(latent_full, lax.axis_index("ctx") * tokens, tokens, 0)
    noise_slope = (-(noise_root / signal_root) * latent_slope).astype(jnp.bfloat16)
    modulated_slope = (
        jnp.einsum("tp,dp->td", noise_slope, final_weight, preferred_element_type=jnp.float32)
        * gain_rows
    )
    residual_slope = (
        modulated_slope
        - jnp.mean(modulated_slope, axis=-1, keepdims=True)
        - unit_rows * jnp.mean(modulated_slope * unit_rows, axis=-1, keepdims=True)
    ) * inverse
    grad_stream = residual_slope.astype(jnp.bfloat16)
    attended_slope = jnp.einsum(
        "td,hd->th", grad_stream, full_weight, preferred_element_type=jnp.float32
    ).astype(jnp.bfloat16)
    slope_heads = attended_slope.reshape(tokens, KV_HEADS, per_group, HEAD)
    row_delta = jnp.transpose(
        jnp.sum(
            slope_heads.astype(jnp.float32)
            * attended.reshape(tokens, KV_HEADS, per_group, HEAD).astype(jnp.float32),
            axis=-1,
        ),
        (1, 2, 0),
    )
    start_grad = jnp.zeros(shape_heads + (HEAD,), jnp.float32)
    backward_key_piece = lax.all_gather(keys[0], "ctx", axis=0, tiled=True)
    backward_value_piece = lax.all_gather(values[0], "ctx", axis=0, tiled=True)

    def backward_advance(current):
        row_count = backward_key_piece.shape[0]
        scores = key_scores(backward_key_piece)
        weights_rows = jnp.exp(scores - log_total[..., None])
        slopes = jnp.einsum(
            "tkgd,skd->kgts",
            slope_heads,
            backward_value_piece.reshape(row_count, KV_HEADS, HEAD),
            preferred_element_type=jnp.float32,
        )
        score_slope = (weights_rows * (slopes - row_delta[..., None])).astype(jnp.bfloat16)
        return jnp.einsum(
            "kgts,skd->kgtd",
            score_slope,
            backward_key_piece.reshape(row_count, KV_HEADS, HEAD),
            preferred_element_type=jnp.float32,
        )

    query_slope = lax.cond(jnp.int32(0) < clip_length, backward_advance, keep_state, start_grad)
    grad_queries = (
        jnp.transpose(query_slope, (2, 0, 1, 3)).reshape(tokens, HEADS * HEAD) / math.sqrt(HEAD)
    ).astype(jnp.bfloat16)
    return (jnp.reshape(reward, (1,)), grad_stream[None], grad_queries[None])


def solution(mesh):
    return jax.shard_map(
        per_device,
        mesh=mesh,
        in_specs=(
            P("dp", "ctx", None),
            P("dp", "ctx", None),
            P("dp", "ctx", None),
            P("dp", "ctx", None),
            P("dp"),
            P("dp", None),
            P("dp", None),
            P("ctx", "dp"),
            P(),
            P("dp", "ctx", None),
            P("dp"),
            P("dp", None),
            P(),
            P(),
            P(None, "ctx"),
            P("ctx", None),
            P(),
            P(),
        ),
        out_specs=(P("dp"), P("dp", "ctx", None), P("dp", "ctx", None)),
        check_vma=False,
    )
```

profile of v0, /device:TPU:1, one launch (start us, length us, event | category | flops | bytes accessed | tf_op | source)
XLA Modules:
  0.0 345.5 jit_solution(14946563173344470295)
XLA Ops:
  8.0 78.0 %all-gather.5.cloned.1.call-done = bf16[512,4096]{1,0:T(8,128)(2,1)} async-done(((bf16[512,512]{1,0:T(8,128)(2,1)}), bf16[512,4096]{1,0:T(8,128)(2,1)}) %all-gather.5.cloned.1.call-update) | async-done | bytes 4194320 | tf_op jit(solution)/shard_map/all_gather | solution.py:106
  88.6 8.9 %all-gather = bf16[1,512,512]{2,1,0:T(8,128)(2,1)} all-gather(bf16[1,128,512]{2,1,0:T(8,128)(2,1)S(1)} %copy-done.12), channel_id=2, replica_groups=mesh['dp'=8,'ctx'=4] {'ctx'}, dimensions={1}, use_global_device_ids=true | all-gather | bytes 655360 | tf_op jit(solution)/shard_map/all_gather | solution.py:75
  97.5 10.7 %all-gather.1 = bf16[1,512,512]{2,1,0:T(8,128)(2,1)} all-gather(bf16[1,128,512]{2,1,0:T(8,128)(2,1)S(1)} %copy-done.13), channel_id=3, replica_groups=mesh['dp'=8,'ctx'=4] {'ctx'}, dimensions={1}, use_global_device_ids=true | all-gather | bytes 655360 | tf_op jit(solution)/shard_map/all_gather | solution.py:76
  108.2 7.9 %conditional.2 = (f32[4,4,128]{2,1,0:T(4,128)S(1)}, f32[4,4,128]{2,1,0:T(4,128)S(1)}, f32[4,4,128]{2,1,0:T(4,128)S(1)}, f32[4,4,128,128]{2,3,1,0:T(8,128)S(1)}) conditional(s32[]{:T(128)} %convert_element_type.107, () %tuple.24, (s32[]{:T(128)}, bf16[512,512]{1,0:T(8,128)(2,1)}, bf16[128,4,4,128]{0,3,2,1:T(8,128)(2,1)}, ...), branch_computations={%region_0.0_spmd, %region_1.4_spmd} | conditional | flops 548669952 | bytes 19548252 | solution.py:97
  108.2 1.2 reshape.141
  110.0 1.2 reshape.140
  111.2 1.8 bitcast_reduce_fusion
  114.0 1.4 fusion.9
  117.7 78.0 %all-gather.7.cloned.1.call-done = bf16[2048,4096]{1,0:T(8,128)(2,1)} async-done(((bf16[512,4096]{1,0:T(8,128)(2,1)}), bf16[2048,4096]{1,0:T(8,128)(2,1)}) %all-gather.7.cloned.1.call-update) | async-done | bytes 16777232 | tf_op jit(solution)/shard_map/all_gather | solution.py:107
  195.7 8.6 %fusion.90 = (f32[128]{0:T(128)S(1)}, f32[128,4096]{1,0:T(8,128)S(1)}) fusion(bf16[128,2048]{0,1:T(8,128)(2,1)} %bitcast.75, bf16[2048,4096]{1,0:T(8,128)(2,1)} %all-gather.7.cloned.1.call-done, bf16[1,128,4096]{2,1,0:T(8,128)(2,1)} %param.22), kind=kOutput, calls=%fused_computation.131 | convolution fusion | flops 2149056512 | bytes 20447744 | tf_op jit(solution)/shard_map/dot_general | solution.py:108
  205.8 5.5 %all_gather.21 = bf16[512,128]{1,0:T(8,128)(2,1)S(1)} all-gather(bf16[128,128]{1,0:T(8,128)(2,1)S(1)} %fusion.40), channel_id=1, replica_groups=mesh['dp'=8,'ctx'=4] {'ctx'}, dimensions={0}, use_global_device_ids=true | all-gather | bytes 163840 | tf_op jit(solution)/shard_map/all_gather | solution.py:121
  212.2 1.6 multiply_reduce_fusion.6
  214.9 3.7 %fusion.57 = f32[256,1536]{1,0:T(8,128)S(1)} fusion(bf16[1408,1536]{1,0:T(8,128)(2,1)} %param.36, f32[1408]{0:T(1024)S(1)} %copy-done.17, f32[256,1408]{1,0:T(8,128)S(1)} %get-tuple-element.94, f32[256]{0:T(256)S(1)} %add_sqrt_fusion.1), kind=kOutput, calls=%fused_computation.88 | convolution fusion | flops 1108377600 | bytes 7346688 | tf_op jit(solution)/shard_map/dot_general | solution.py:128
  218.7 1.2 copy-done.33
  219.9 2.4 convolution_convert_fusion.1
  222.5 30.3 %all-reduce.3.cloned.1.call-done = bf16[256,1408]{1,0:T(8,128)(2,1)} async-done(((bf16[256,1408]{1,0:T(8,128)(2,1)}), bf16[256,1408]{1,0:T(8,128)(2,1)}) %all-reduce.3.cloned.1.call-update) | async-done | bytes 720912 | tf_op jit(solution)/shard_map/psum | solution.py:132
  252.9 2.0 multiply_reduce_fusion.5
  255.1 2.2 multiply_reduce_fusion.3
  257.8 8.4 %convolution_convert_fusion = bf16[256,1408]{1,0:T(8,128)(2,1)} fusion(bf16[1408,1536]{1,0:T(8,128)(2,1)} %param.36, f32[256,1536]{1,0:T(8,128)} %copy-done.33, bf16[1536,1408]{1,0:T(8,128)(2,1)} %param.37, f32[256,1408]{1,0:T(8,128)} %get-tuple-element.87, f32[256]{0:T(256)S(1)} %broadcast_multiply_fusion.1, f32[1408]{0:T(1024)S(1)} %multiply_multiply_fusion.2, ...), kind=kOutput, calls=%fused_computation.38 | convolution fusion | flops 2224259072 | bytes 12393984 | tf_op jit(solution)/shard_map/rh,wh->rw/dot_general | solution.py:150
  266.9 33.8 %all-reduce.5.cloned.1.call-done = bf16[256,1408]{1,0:T(8,128)(2,1)} async-done(((bf16[256,1408]{1,0:T(8,128)(2,1)}), bf16[256,1408]{1,0:T(8,128)(2,1)}) %all-reduce.5.cloned.1.call-update) | async-done | bytes 720912 | tf_op jit(solution)/shard_map/psum | solution.py:149
  300.8 2.1 multiply_reduce_fusion.2
  302.9 2.7 fusion.65
  305.7 1.8 scatter_custom_fusion
  307.5 1.4 fusion.86
  309.0 1.7 multiply_convert_fusion
  310.6 11.8 %convolution_convert_fusion.2 = bf16[128,2048]{1,0:T(8,128)(2,1)S(1)} fusion(bf16[128,4096]{1,0:T(8,128)(2,1)} %multiply_convert_fusion, bf16[2048,4096]{1,0:T(8,128)(2,1)} %all-gather.7.cloned.1.call-done), kind=kOutput, calls=%fused_computation.40 | convolution fusion | flops 2147745792 | bytes 18350080 | tf_op jit(solution)/shard_map/td,hd->th/dot_general | solution.py:181
  324.0 12.2 %conditional.3 = (f32[4,4,128,128]{3,2,1,0:T(8,128)S(1)}) conditional(s32[]{:T(128)} %convert_element_type.107, () %tuple.26, (s32[]{:T(128)}, bf16[512,512]{1,0:T(8,128)(2,1)}, bf16[128,4,4,128]{0,3,2,1:T(8,128)(2,1)}, f32[4,4,128]{2,1,0:T(4,128)S(1)}, f32[4,4,128]{2,1,0:T(4,128)S(1)}, /*index=5*/bf16[512,512]{1,0:T(8,128)(2,1)}, ...), branch_computations={%region_17.18_spmd, %region_18.19_spmd} | conditional | flops 811600384 | bytes 14214156 | solution.py:215
  325.0 2.0 reshape.143
  327.0 1.2 reshape.142
  328.1 3.7 %fusion.27 = f32[4,512,128,4]{2,1,3,0:T(8,128)} fusion(bf16[128,4,4,128]{0,3,2,1:T(8,128)(2,1)} %get-tuple-element.74, bf16[512,4,128,1]{2,1,0,3:T(4,128)(2,1)S(1)} %bitcast.76), kind=kOutput, calls=%fused_computation.31 | convolution fusion | flops 268435456 | bytes 5242880 | tf_op jit(solution)/shard_map/cond/branch_1_fun/tkgd,skd->kgts/dot_general | solution.py:60
  331.9 4.3 %fusion.21 = f32[4,4,128,128]{3,2,1,0:T(8,128)S(1)} fusion(f32[4,512,128,4]{2,1,3,0:T(8,128)} %fusion.27, f32[4,4,128]{2,1,0:T(4,128)S(1)} %copy.63, f32[4,4,128]{2,1,0:T(4,128)S(1)} %add.87, pred[512]{0:T(512)(128)(4,1)S(1)} %iota_compare_fusion.1, bf16[512,4,128,1]{2,1,0,3:T(4,128)(2,1)} %bitcast.81, bf16[128,4,4,128]{3,2,1,0:T(4,128)(2,1)S(1)} %get-tuple-element.78, ...), kind=kOutput, calls=%fused_computation.27 | convolution fusion | flops 543162368 | bytes 6832640 | tf_op jit(solution)/shard_map/cond/branch_1_fun/kgts,skd->kgtd/dot_general | solution.py:208
  336.7 1.2 convert_element_type.129
  (110 shorter events, 13.1 us)
Async XLA Ops:
  7.2 198.1 %copy-start = (bf16[4096,128]{1,0:T(8,128)(2,1)S(1)}, bf16[4096,128]{1,0:T(8,128)(2,1)}, u32[]{:S(2)}) copy-start(bf16[4096,128]{1,0:T(8,128)(2,1)} %param.30) | copy-start | bytes 3145732
  7.2 78.8 %all-gather.5.cloned.1.call-start = ((), (), s32[]{:S(2)}) async-start(), calls=%async_computation | async-start | bytes 4718592 | tf_op jit(solution)/shard_map/all_gather | solution.py:106
  7.9 187.7 %all-gather.7.cloned.1.call-start = ((), (), s32[]{:S(2)}) async-start(), calls=%async_computation.1 | async-start | bytes 20971520 | tf_op jit(solution)/shard_map/all_gather | solution.py:107
  86.0 1.6 copy-start.8
  86.0 2.6 copy-start.12
  86.0 11.5 %copy-start.13 = (bf16[1,128,512]{2,1,0:T(8,128)(2,1)S(1)}, bf16[1,128,512]{2,1,0:T(8,128)(2,1)}, u32[]{:S(2)}) copy-start(bf16[1,128,512]{2,1,0:T(8,128)(2,1)} %param.25) | copy-start | bytes 393220
  86.0 166.8 %all-reduce.3.cloned.1.call-start = ((), (), s32[]{:S(2)}) async-start(), calls=%async_computation.2 | async-start | bytes 1441792 | tf_op jit(solution)/shard_map/psum | solution.py:132
  108.2 8.0 %copy-start.28 = (s32[1,256]{1,0:T(1,128)S(1)}, s32[1,256]{1,0:T(1,128)}, u32[]{:S(2)}) copy-start(s32[1,256]{1,0:T(1,128)} %param.33) | copy-start | bytes 3076
  116.1 79.5 %copy-start.4 = (f32[4,4,128,128]{2,3,1,0:T(8,128)}, f32[4,4,128,128]{2,3,1,0:T(8,128)S(1)}, u32[]{:S(2)}) copy-start(f32[4,4,128,128]{2,3,1,0:T(8,128)S(1)} %get-tuple-element.80) | copy-start | bytes 3145732
  116.1 1.5 copy-start.16
  205.8 9.1 %copy-start.17 = (f32[1408]{0:T(1024)S(1)}, f32[1408]{0:T(1024)}, u32[]{:S(2)}) copy-start(f32[1408]{0:T(1024)} %param.35) | copy-start | bytes 16900
  212.2 7.7 %slice-start = ((s8[4325376]{0:T(1024)(128)(4,1)}), s8[4194304]{0:T(1024)(128)(4,1)S(1)}, s32[]{:S(2)}) async-start(s8[4325376]{0:T(1024)(128)(4,1)} %bitcast.87), calls=%async_computation.4 | async-start | bytes 8388608
  213.8 1.1 copy-start.1
  213.8 1.1 copy-start.21
  214.9 4.9 %slice-start.1 = ((s8[4325376]{0:T(1024)(128)(4,1)}), s8[131072]{0:T(1024)(128)(4,1)S(1)}, s32[]{:S(2)}) async-start(s8[4325376]{0:T(1024)(128)(4,1)} %bitcast.87), calls=%async_computation.5 | async-start | bytes 262144
  218.7 1.2 copy-start.33
  219.9 2.6 copy-start.14
  219.9 2.6 copy-start.15
  222.3 78.5 %all-reduce.5.cloned.1.call-start = ((), (), s32[]{:S(2)}) async-start(), calls=%async_computation.3 | async-start | bytes 1441792 | tf_op jit(solution)/shard_map/psum | solution.py:149
  252.9 2.0 copy-start.2
  252.9 2.2 copy-start.6
  255.1 2.2 copy-start.23
  266.1 36.7 %copy-start.9 = (bf16[128,1408]{1,0:T(8,128)(2,1)S(1)}, bf16[128,1408]{1,0:T(8,128)(2,1)}, u32[]{:S(2)}) copy-start(bf16[128,1408]{1,0:T(8,128)(2,1)} %param.34) | copy-start | bytes 1081348
  300.7 2.1 copy-start.3
  300.7 2.2 copy-start.7
  300.7 2.2 copy-start.18
  300.7 2.2 copy-start.22
  300.7 2.2 copy-start.24
  300.7 2.2 copy-start.30
  307.5 1.4 copy-start.20
  307.5 1.4 copy-start.27
  322.4 1.2 copy-start.5
  (8 other events, 5.8 us)
Sparse Core Ops, SparseCore 0:
  10.0 75.9 all-gather.4
  87.6 108.0 all-gather.6
  222.4 30.4 all-reduce.2
  266.3 34.3 all-reduce.4
where the time goes:
time: 348 us; the launch traced here: 346 us
  waiting for transfers between devices  221 us (64%)
  matrix products  52.3 us (15%)
  blocking collectives  25.1 us (7%)
  between operations  17.5 us (5%)
  local copies, waits for them, and re-layouts  15.4 us (4%)
  other arithmetic  13.7 us (4%)
    all_gather x1, waiting for transfers between devices, per_device(): column_full = lax.all_gather(out_weight, 'dp', axis=1, tiled=True)  78 us
    all_gather x1, waiting for transfers between devices, per_device(): full_weight = lax.all_gather(column_full, 'ctx', axis=0, tiled=True)  78 us
    psum x1, waiting for transfers between devices, per_device(): lax.psum(jnp.einsum('rh,wh->rw', hidden_slope, up_weight, preferred_eleme...  33.8 us
    psum x1, waiting for transfers between devices, per_device(): lax.psum(jnp.dot(active, down_weight, preferred_element_type=jnp.float32)...  30.3 us
    dot_general x1, matrix products, per_device(): jnp.einsum('td,hd->th', grad_stream, full_weight, preferred_element_type=...  11.8 us
    all_gather x1, blocking collectives, per_device(): value_piece = lax.all_gather(values[0], 'ctx', axis=0, tiled=True)  10.7 us
    all_gather x1, blocking collectives, per_device(): key_piece = lax.all_gather(keys[0], 'ctx', axis=0, tiled=True)  8.9 us
    dot_general x1, matrix products, per_device(): jnp.dot(attended, full_weight, preferred_element_type=jnp.float32)  8.59 us
  transfers between devices with their start and end apart: 4, of which 4 were waited for; matrix products, arithmetic and copies ran while one was open for 3% of the time, Pallas kernels for 0%

commit v1 on v0

v1 whole, which is shorter than its diff:
```python
import functools
import math

import jax
import jax.numpy as jnp
from jax import lax
from jax.experimental import pallas as pl
from jax.experimental.pallas import tpu as pltpu
from jax.sharding import PartitionSpec as P

HEADS = 16
KV_HEADS = 4
HEAD = 128
PATCH = 128


MASKED = -1e30
LOSS_SCALE = 16.0
EPSILON = 1e-06
MESH = pl.DeviceIdType.MESH
VMEM_SPEC = pl.BlockSpec(memory_space=pltpu.VMEM)


def remote(src, dst, send, recv, axis, peer):
    return pltpu.make_async_remote_copy(
        src_ref=src,
        dst_ref=dst,
        send_sem=send,
        recv_sem=recv,
        device_id={axis: peer},
        device_id_type=MESH,
    )


def greet(axis, peers):
    barrier = pltpu.get_barrier_semaphore()
    for peer in peers:
        pl.semaphore_signal(barrier, inc=1, device_id={axis: peer}, device_id_type=MESH)
    pl.semaphore_wait(barrier, len(peers))


def params(collective_id):
    return pltpu.CompilerParams(
        collective_id=collective_id, has_side_effects=True, vmem_limit_bytes=48 * 1024 * 1024
    )


def swap_start(n, src, dst, send, recv):
    me = lax.axis_index("ctx")
    copies = []
    for k in range(1, n):
        peer = lax.rem(me + k, n)
        copy = remote(src.at[peer], dst.at[me], send.at[k - 1], recv.at[k - 1], "ctx", peer)
        copy.start()
        copies.append(copy)
    return copies


def swap_kernel(n, src, dst, send, recv, local):
    me = lax.axis_index("ctx")
    greet("ctx", [lax.rem(me + k, n) for k in range(1, n)])
    copies = swap_start(n, src, dst, send, recv)
    own = pltpu.make_async_copy(src.at[me], dst.at[me], local)
    own.start()
    own.wait()
    for copy in copies:
        copy.wait()


def swap(pieces, n, collective_id):
    return pl.pallas_call(
        functools.partial(swap_kernel, n),
        out_shape=jax.ShapeDtypeStruct(pieces.shape, pieces.dtype),
        in_specs=[VMEM_SPEC],
        out_specs=VMEM_SPEC,
        scratch_shapes=[
            pltpu.SemaphoreType.DMA((n - 1,)),
            pltpu.SemaphoreType.DMA((n - 1,)),
            pltpu.SemaphoreType.DMA,
        ],
        compiler_params=params(collective_id),
    )(pieces)


def front_kernel(
    n, dp_n, src, weight, dst, full, send, recv, local, up_s, up_r, dn_s, dn_r, ac_s, ac_r
):
    me = lax.axis_index("ctx")
    mine = lax.axis_index("dp")
    n_out = dp_n // 2
    outer, inner = mine // 2, lax.rem(mine, 2)
    across = outer * 2 + 1 - inner
    above, below = lax.rem(mine + 2, dp_n), lax.rem(mine + dp_n - 2, dp_n)
    has_up, has_down = outer + 1 < n_out, outer >= 1
    width = weight.shape[1]

    def block(index):
        return full.at[:, pl.ds(pl.multiple_of(index * width, width), width)]

    barrier = pltpu.get_barrier_semaphore()
    for k in range(1, n):
        pl.semaphore_signal(
            barrier, inc=1, device_id={"ctx": lax.rem(me + k, n)}, device_id_type=MESH
        )
    for peer in (across, above, below):
        pl.semaphore_signal(barrier, inc=1, device_id={"dp": peer}, device_id_type=MESH)
    pl.semaphore_wait(barrier, n + 2)
    copies = swap_start(n, src, dst, send, recv)

    def up(source, index, step):
        return remote(source, block(index), up_s.at[step], up_r.at[step], "dp", above)

    def down(source, index, step):
        return remote(source, block(index), dn_s.at[step], dn_r.at[step], "dp", below)

    def cross(source, index, step):
        return remote(source, block(index), ac_s.at[step], ac_r.at[step], "dp", across)

    pl.when(has_up)(lambda: up(weight, mine, 0).start())
    pl.when(has_down)(lambda: down(weight, mine, 0).start())
    cross(weight, mine, 0).start()
    own = pltpu.make_async_copy(src.at[me], dst.at[me], local.at[0])
    own.start()
    own_weight = pltpu.make_async_copy(weight, block(mine), local.at[1])
    own_weight.start()
    for step in range(1, n_out):
        low, high = mine - 2 * step, mine + 2 * step

        @pl.when(outer >= step)
        def _():
            up(block(low), low, step - 1).wait_recv()
            pl.when(has_up)(lambda: up(block(low), low, step).start())
            cross(block(low), low, step).start()

        @pl.when(outer + step < n_out)
        def _():
            down(block(high), high, step - 1).wait_recv()
            pl.when(has_down)(lambda: down(block(high), high, step).start())
            cross(block(high), high, n_out + step).start()

    own.wait()
    own_weight.wait()
    for copy in copies:
        copy.wait()
    pl.when(has_up)(lambda: up(weight, mine, 0).wait_send())
    pl.when(has_down)(lambda: down(weight, mine, 0).wait_send())
    cross(weight, mine, 0).wait()
    for step in range(1, n_out):
        low, high = mine - 2 * step, mine + 2 * step

        @pl.when(outer >= step)
        def _():
            pl.when(has_up)(lambda: up(block(low), low, step).wait_send())
            cross(block(low), low, step).wait()

        @pl.when(outer + step < n_out)
        def _():
            pl.when(has_down)(lambda: down(block(high), high, step).wait_send())
            cross(block(high), high, n_out + step).wait()


def front(pieces, weight, n, dp_n, collective_id):
    dma = pltpu.SemaphoreType.DMA
    n_out = dp_n // 2
    return pl.pallas_call(
        functools.partial(front_kernel, n, dp_n),
        out_shape=(
            jax.ShapeDtypeStruct(pieces.shape, pieces.dtype),
            jax.ShapeDtypeStruct((weight.shape[0], weight.shape[1] * dp_n), weight.dtype),
        ),
        in_specs=[VMEM_SPEC] * 2,
        out_specs=(VMEM_SPEC, VMEM_SPEC),
        scratch_shapes=[dma((n - 1,)), dma((n - 1,)), dma((2,))]
        + [dma((n_out,))] * 4
        + [dma((2 * n_out,))] * 2,
        compiler_params=params(collective_id),
    )(pieces, weight)


def collect_kernel(n, src, dst, send, recv, local):
    me = lax.axis_index("ctx")
    n_out = n // 2
    outer, core = me // 2, lax.rem(me, 2)
    partner = outer * 2 + 1 - core
    peers = [lax.rem(outer + k, n_out) * 2 + core for k in range(1, n_out)]
    greet("ctx", peers + [partner])
    copies = []
    for k, peer in enumerate(peers):
        copy = remote(src, dst.at[me], send.at[k + 1], recv.at[k + 1], "ctx", peer)
        copy.start()
        copies.append(copy)
    first = remote(src, dst.at[me], send.at[0], recv.at[0], "ctx", partner)
    first.start()
    own = pltpu.make_async_copy(src, dst.at[me], local)
    own.start()
    relays = []
    for k, copy in enumerate(copies):
        copy.wait_recv()
        held = lax.rem(outer + n_out - k - 1, n_out) * 2 + core
        relay = remote(
            dst.at[held], dst.at[held], send.at[n_out + k], recv.at[n_out + k], "ctx", partner
        )
        relay.start()
        relays.append(relay)
    own.wait()
    first.wait()
    for copy in copies:
        copy.wait_send()
    for relay in relays:
        relay.wait()


def collect(piece, n, collective_id):
    return pl.pallas_call(
        functools.partial(collect_kernel, n),
        out_shape=jax.ShapeDtypeStruct((n,) + piece.shape, piece.dtype),
        in_specs=[VMEM_SPEC],
        out_specs=VMEM_SPEC,
        scratch_shapes=[
            pltpu.SemaphoreType.DMA((n,)),
            pltpu.SemaphoreType.DMA((n,)),
            pltpu.SemaphoreType.DMA,
        ],
        compiler_params=params(collective_id),
    )(piece)


def reduce_kernel(n, src, dst, near, paired, far, near_s, near_r, far_s, far_r):
    me = lax.axis_index("ctx")
    n_out = n // 2
    outer, core = me // 2, lax.rem(me, 2)
    partner = outer * 2 + 1 - core
    rows = dst.shape[0]
    chunk = 16
    owners = [lax.rem(outer + k, n_out) for k in range(n_out)]
    greet("ctx", [owner * 2 + core for owner in owners[1:]] + [partner])
    nears = {}
    for k in list(range(1, n_out)) + [0]:
        copy = remote(
            src.at[owners[k] * 2 + 1 - core],
            near.at[k],
            near_s.at[k],
            near_r.at[k],
            "ctx",
            partner,
        )
        copy.start()
        nears[k] = copy
    fars = []
    for k in range(1, n_out):
        nears[k].wait_recv()
        source = owners[k] * 2 + core

        @pl.loop(0, rows // chunk)
        def _(r):
            at = pl.ds(pl.multiple_of(r * chunk, chunk), chunk)
            total = src[source, at, :].astype(jnp.float32) + near[k, at, :].astype(jnp.float32)
            paired[k - 1, at, :] = total.astype(jnp.bfloat16)

        copy = remote(
            paired.at[k - 1], far.at[k - 1], far_s.at[k - 1], far_r.at[k - 1], "ctx", source
        )
        copy.start()
        fars.append(copy)
    nears[0].wait_recv()
    for copy in fars:
        copy.wait_recv()

    @pl.loop(0, rows // chunk)
    def _(r):
        at = pl.ds(pl.multiple_of(r * chunk, chunk), chunk)
        total = src[me, at, :].astype(jnp.float32) + near[0, at, :].astype(jnp.float32)
        for k in range(n_out - 1):
            total = total + far[k, at, :].astype(jnp.float32)
        dst[at, :] = total

    for k in range(n_out):
        nears[k].wait_send()
    for copy in fars:
        copy.wait_send()


def reduce(pieces, n, collective_id):
    shape = pieces.shape[1:]
    n_out = n // 2
    dma = pltpu.SemaphoreType.DMA
    return pl.pallas_call(
        functools.partial(reduce_kernel, n),
        out_shape=jax.ShapeDtypeStruct(shape, jnp.float32),
        in_specs=[VMEM_SPEC],
        out_specs=VMEM_SPEC,
        scratch_shapes=[
            pltpu.VMEM((n_out,) + shape, jnp.bfloat16),
            pltpu.VMEM((n_out - 1,) + shape, jnp.bfloat16),
            pltpu.VMEM((n_out - 1,) + shape, jnp.bfloat16),
            dma((n_out,)),
            dma((n_out,)),
            dma((n_out - 1,)),
            dma((n_out - 1,)),
        ],
        compiler_params=params(collective_id),
    )(pieces)


def plan(noise_step):
    phase = (noise_step.astype(jnp.float32) / 1000.0 + 0.008) / 1.008 * (math.pi / 2.0)
    signal_root = jnp.cos(phase)
    return (signal_root, jnp.sqrt(1.0 - signal_root * signal_root))


def gelu_slope(hidden, upstream):
    return jax.vjp(lambda argument: jax.nn.gelu(argument, approximate=True), hidden)[1](upstream)[0]


def matmul(subscripts, left, right):
    return jnp.einsum(subscripts, left, right, preferred_element_type=jnp.float32)


def per_device(
    n,
    dp_n,
    stream,
    queries,
    keys,
    values,
    clip_lengths,
    mod_shift,
    mod_scale,
    out_weight,
    final_weight,
    noisy_latents,
    timestep,
    crop_map,
    embed_weight,
    pre_gain,
    up_weight,
    down_weight,
    post_gain,
    head_weight,
):
    tokens = queries.shape[1]
    sequence = tokens * n
    width = stream.shape[2]
    heads = HEADS // n
    per_group = HEADS // KV_HEADS
    me = lax.axis_index("ctx")
    clip_length = clip_lengths[0]

    groups = [(c * heads) // per_group for c in range(n)]
    pieces = jnp.stack(
        [
            jnp.concatenate(
                [
                    queries[0, :, c * heads * HEAD : (c + 1) * heads * HEAD],
                    keys[0, :, groups[c] * HEAD : (groups[c] + 1) * HEAD],
                    values[0, :, groups[c] * HEAD : (groups[c] + 1) * HEAD],
                ],
                axis=-1,
            )
            for c in range(n)
        ]
    )
    swapped, weight = front(pieces, out_weight, n, dp_n, 0)
    swapped = swapped.reshape(sequence, (heads + 2) * HEAD)
    query_heads = swapped[:, : heads * HEAD].reshape(sequence, heads, HEAD)
    key_rows = swapped[:, heads * HEAD : (heads + 1) * HEAD]
    value_rows = swapped[:, (heads + 1) * HEAD :]

    is_live = jnp.arange(sequence, dtype=jnp.int32) < clip_length
    scores = matmul("thd,sd->hts", query_heads, key_rows) / math.sqrt(HEAD)
    scores = jnp.where(is_live, scores, MASKED)
    highest = jnp.max(scores, axis=-1)
    weights_rows = jnp.exp(scores - highest[..., None])
    denominator = jnp.sum(weights_rows, axis=-1)
    numerator = matmul("hts,sd->htd", weights_rows.astype(jnp.bfloat16), value_rows)
    attended_heads = (numerator / denominator[..., None]).astype(jnp.bfloat16)
    attended = jnp.transpose(attended_heads, (1, 0, 2)).reshape(sequence, heads * HEAD)
    log_total = highest + jnp.log(denominator)

    product = matmul("tr,rc->tc", attended, weight).astype(jnp.bfloat16)
    residual = stream[0].astype(jnp.float32) + reduce(product.reshape(n, tokens, width), n, 1)
    centred = residual - jnp.mean(residual, axis=-1, keepdims=True)
    inverse = lax.rsqrt(jnp.mean(centred * centred, axis=-1, keepdims=True) + EPSILON)
    unit_rows = centred * inverse
    gain_rows = 1.0 + mod_scale[0]
    modulated = (unit_rows * gain_rows + mod_shift[0]).astype(jnp.bfloat16)
    predicted = jnp.dot(modulated, final_weight, preferred_element_type=jnp.float32)
    signal_root, noise_root = plan(timestep[0])
    denoised = (
        (noisy_latents[0].astype(jnp.float32) - noise_root * predicted) / signal_root
    ).astype(jnp.bfloat16)

    final_wide = final_weight.astype(jnp.float32)
    gained = final_wide * gain_rows[:, None]
    gained_mean = jnp.mean(gained, axis=0)
    along_unit = predicted - jnp.sum(final_wide * mod_shift[0][:, None], axis=0)
    bundle = jnp.concatenate(
        [
            denoised,
            along_unit.astype(jnp.bfloat16),
            jnp.broadcast_to(inverse, (tokens, PATCH)).astype(jnp.bfloat16),
        ],
        axis=-1,
    )
    bundles = collect(bundle, n, 2).reshape(sequence, 3 * PATCH)
    gathered = bundles[:, :PATCH]
    unit_full = lax.all_gather(unit_rows.astype(jnp.bfloat16), "ctx", axis=0, tiled=True)
    unit_out = matmul("tc,rc->tr", unit_full, weight)
    gained_out = matmul("rc,cp->rp", weight, gained.astype(jnp.bfloat16)).astype(jnp.bfloat16)
    weight_sum = jnp.sum(weight.astype(jnp.float32), axis=-1)

    crop_rows = crop_map[0]
    crop_tokens = jnp.take(gathered, crop_rows, axis=0)
    embedded = jnp.dot(crop_tokens, embed_weight, preferred_element_type=jnp.float32)
    first_root = jnp.sqrt(jnp.mean(embedded * embedded, axis=-1, keepdims=True) + EPSILON)
    first_unit = embedded / first_root
    normed = (first_unit * pre_gain).astype(jnp.bfloat16)
    hidden = jnp.dot(normed, up_weight, preferred_element_type=jnp.float32)
    active = jax.nn.gelu(hidden, approximate=True).astype(jnp.bfloat16)
    row_total, reward_width = embedded.shape
    rows = row_total // n

    def own_rows(whole):
        return lax.dynamic_slice_in_dim(whole, me * rows, rows, 0)

    head_slope = -(LOSS_SCALE / row_total) * head_weight * post_gain
    down_part = jnp.dot(active, down_weight, preferred_element_type=jnp.float32)
    summed = own_rows(embedded) + reduce(
        down_part.astype(jnp.bfloat16).reshape(n, rows, reward_width), n, 3
    )
    second_root = jnp.sqrt(jnp.mean(summed * summed, axis=-1, keepdims=True) + EPSILON)
    second_unit = summed / second_root
    row_rewards = jnp.sum(second_unit * post_gain * head_weight, axis=-1, keepdims=True)
    summed_slope = (
        head_slope - second_unit * jnp.mean(head_slope * second_unit, axis=-1, keepdims=True)
    ) / second_root
    summed_slopes = collect(summed_slope.astype(jnp.bfloat16), n, 4).reshape(
        row_total, reward_width
    )
    active_slope = matmul("rw,hw->rh", summed_slopes, down_weight)
    hidden_slope = gelu_slope(hidden, active_slope).astype(jnp.bfloat16)
    up_part = matmul("rh,wh->rw", hidden_slope, up_weight)
    normed_slope = (
        reduce(up_part.astype(jnp.bfloat16).reshape(n, rows, reward_width), n, 5) * pre_gain
    )
    own_unit = own_rows(first_unit)
    embed_slope = (
        summed_slope
        + (normed_slope - own_unit * jnp.mean(normed_slope * own_unit, axis=-1, keepdims=True))
        / own_rows(first_root)
    )
    token_slope = matmul("rw,pw->rp", embed_slope.astype(jnp.bfloat16), embed_weight)
    token_slopes = collect(
        jnp.concatenate([token_slope, jnp.broadcast_to(row_rewards, (rows, PATCH))], axis=-1), n, 6
    ).reshape(row_total, 2 * PATCH)
    reward = jnp.mean(token_slopes[:, PATCH])
    latent_full = (
        jnp.zeros((sequence, PATCH), jnp.float32).at[crop_rows].add(token_slopes[:, :PATCH])
    )
    noise_slopes = (-(noise_root / signal_root) * latent_full).astype(jnp.bfloat16)
    noise_slope = lax.dynamic_slice_in_dim(noise_slopes, me * tokens, tokens, 0)
    modulated_slope = matmul("tp,dp->td", noise_slope, final_weight) * gain_rows
    residual_slope = (
        modulated_slope
        - jnp.mean(modulated_slope, axis=-1, keepdims=True)
        - unit_rows * jnp.mean(modulated_slope * unit_rows, axis=-1, keepdims=True)
    ) * inverse
    grad_stream = residual_slope.astype(jnp.bfloat16)

    noise_wide = noise_slopes.astype(jnp.float32)
    slope_mean = jnp.sum(noise_wide * gained_mean, axis=-1, keepdims=True)
    slope_along = (
        jnp.sum(
            noise_wide * bundles[:, PATCH : 2 * PATCH].astype(jnp.float32), axis=-1, keepdims=True
        )
        / width
    )
    attended_slope = (
        (
            matmul("tp,rp->tr", noise_slopes, gained_out)
            - slope_mean * weight_sum
            - slope_along * unit_out
        )
        * bundles[:, 2 * PATCH : 2 * PATCH + 1].astype(jnp.float32)
    ).astype(jnp.bfloat16)
    slope_heads = attended_slope.reshape(sequence, heads, HEAD)
    row_delta = jnp.sum(
        jnp.transpose(slope_heads, (1, 0, 2)).astype(jnp.float32)
        * attended_heads.astype(jnp.float32),
        axis=-1,
    )
    back_scores = matmul("thd,sd->hts", query_heads, key_rows) / math.sqrt(HEAD)
    back_scores = jnp.where(is_live, back_scores, MASKED)
    back_weights = jnp.exp(back_scores - log_total[..., None])
    slopes = matmul("thd,sd->hts", slope_heads, value_rows)
    score_slope = (back_weights * (slopes - row_delta[..., None])).astype(jnp.bfloat16)
    query_slope = matmul("hts,sd->htd", score_slope, key_rows) / math.sqrt(HEAD)
    by_head = (
        jnp.transpose(query_slope, (1, 0, 2))
        .reshape(n, tokens, heads * HEAD)
        .astype(jnp.bfloat16)
    )
    grad_queries = jnp.transpose(swap(by_head, n, 7), (1, 0, 2)).reshape(tokens, HEADS * HEAD)
    return (jnp.reshape(reward, (1,)), grad_stream[None], grad_queries[None])


def solution(mesh):
    return jax.shard_map(
        functools.partial(per_device, mesh.shape["ctx"], mesh.shape["dp"]),
        mesh=mesh,
        in_specs=(
            P("dp", "ctx", None),
            P("dp", "ctx", None),
            P("dp", "ctx", None),
            P("dp", "ctx", None),
            P("dp"),
            P("dp", None),
            P("dp", None),
            P("ctx", "dp"),
            P(),
            P("dp", "ctx", None),
            P("dp"),
            P("dp", None),
            P(),
            P(),
            P(None, "ctx"),
            P("ctx", None),
            P(),
            P(),
        ),
        out_specs=(P("dp"), P("dp", "ctx", None), P("dp", "ctx", None)),
        check_vma=False,
    )
```

time: 348 us -> 245 us (0.70)
  waiting for transfers between devices: 221 us -> 27.3 us
  Pallas kernels: 0 us -> 131 us
  blocking collectives: 25.1 us -> 0 us
  matrix products: 52.3 us -> 44.1 us
  local copies, waits for them, and re-layouts: 15.4 us -> 9.56 us
    pallas_call x0 -> x8, Pallas kernels: none -> 131 us  [the longest x1 54.3 us: front(): pl.pallas_call(functools.partial(front_kernel, n, dp_n), out_shape=(jax.S...]
    all_gather x2 -> x1, waiting for transfers between devices: 156 us -> 27.3 us  [per_device(): lax.all_gather(unit_rows.astype(jnp.bfloat16), 'ctx', axis=0, tiled=True)]
    psum x2 -> x0, waiting for transfers between devices: 64.2 us -> none  [the longest x1 33.8 us: per_device(): lax.psum(jnp.einsum('rh,wh->rw', hidden_slope, up_weight, preferred_eleme...]
    all_gather x3 -> x0, blocking collectives: 25.1 us -> none  [the longest x1 10.7 us: per_device(): value_piece = lax.all_gather(values[0], 'ctx', axis=0, tiled=True)]
    dot_general x10, matrix products: 46.4 us -> 37.8 us  [the longest x9 33.5 us: matmul(): jnp.einsum(subscripts, left, right, preferred_element_type=jnp.float32)]
    reduce_sum x3 -> x8, other arithmetic: 3.18 us -> 9.83 us  [the longest x1 2.99 us: per_device(): weight_sum = jnp.sum(weight.astype(jnp.float32), axis=-1)]
    reshape x6 -> x0, local copies, waits for them, and re-layouts: 6.31 us -> none  [the longest x2 2.33 us: key_scores(): key_piece.reshape(row_count, KV_HEADS, HEAD)]
  transfers between devices with their start and end apart: 4 -> 1, of which waited for: 4 -> 1; matrix products, arithmetic and copies ran while one was open for 3% -> 2% of each run, Pallas kernels for 0% -> 0%
where the time goes in v1:
time: 245 us
  Pallas kernels  131 us (53%)
  matrix products  44.1 us (18%)
  waiting for transfers between devices  27.3 us (11%)
  between operations  17.9 us (7%)
  other arithmetic  15.1 us (6%)
  local copies, waits for them, and re-layouts  9.56 us (4%)
    pallas_call x1, Pallas kernels, front(): pl.pallas_call(functools.partial(front_kernel, n, dp_n), out_shape=(jax.S...  54.3 us
    pallas_call x3, Pallas kernels, reduce(): pl.pallas_call(functools.partial(reduce_kernel, n), out_shape=jax.ShapeDt...  47.7 us
    dot_general x9, matrix products, matmul(): jnp.einsum(subscripts, left, right, preferred_element_type=jnp.float32)  33.5 us
    all_gather x1, waiting for transfers between devices, per_device(): lax.all_gather(unit_rows.astype(jnp.bfloat16), 'ctx', axis=0, tiled=True)  27.3 us
    pallas_call x3, Pallas kernels, collect(): pl.pallas_call(functools.partial(collect_kernel, n), out_shape=jax.ShapeD...  20.3 us
    pallas_call x1, Pallas kernels, swap(): pl.pallas_call(functools.partial(swap_kernel, n), out_shape=jax.ShapeDtyp...  8.31 us
  transfers between devices with their start and end apart: 1, of which 1 were waited for; matrix products, arithmetic and copies ran while one was open for 2% of the time, Pallas kernels for 0%

profile of v1, /device:TPU:1, one launch (start us, length us, event | category | flops | bytes accessed | tf_op | source)
XLA Modules:
  0.0 244.6 jit_solution(7172794666821662405)
XLA Ops:
  7.2 1.2 slice_bitcast_fusion.5
  10.3 54.3 %shard_map.193 = (bf16[4,128,768]{2,1,0:T(8,128)(2,1)S(1)}, bf16[512,4096]{1,0:T(8,128)(2,1)}) custom-call(bf16[4,128,768]{2,1,0:T(8,128)(2,1)S(1)} %pad_maximum_fusion.src, bf16[512,512]{1,0:T(8,128)(2,1)S(1)} %copy-done.1), custom_call_target="tpu_custom_call" | custom-call | tf_op jit(solution)/shard_map/pallas_call | solution.py:165
  66.3 0.9 fusion.4
  67.2 1.0 copy-done.4
  68.2 2.3 fusion.32
  70.5 4.4 %convolution_convert_fusion = bf16[512,4096]{1,0:T(8,128)(2,1)} fusion(bf16[512,512]{0,1:T(8,128)(2,1)S(1)} %bitcast.162, bf16[512,4096]{1,0:T(8,128)(2,1)S(1)} %copy-done.5), kind=kOutput, calls=%fused_computation.3 | convolution fusion | flops 2149580800 | bytes 8912896 | tf_op jit(solution)/shard_map/tr,rc->tc/dot_general | solution.py:316
  75.0 32.0 %shard_map.194 = f32[128,4096]{1,0:T(8,128)S(1)} custom-call(bf16[4,128,4096]{2,1,0:T(8,128)(2,1)} %bitcast.157), custom_call_target="tpu_custom_call" | custom-call | tf_op jit(solution)/shard_map/pallas_call | solution.py:287
  107.4 1.3 copy-done.2
  109.9 2.2 fusion.6
  112.1 2.2 fusion.60
  114.4 6.4 %shard_map.195 = bf16[4,128,384]{2,1,0:T(8,128)(2,1)S(1)} custom-call(bf16[128,384]{1,0:T(8,128)(2,1)S(1)} %pad_maximum_fusion.1.src), custom_call_target="tpu_custom_call" | custom-call | tf_op jit(solution)/shard_map/pallas_call | solution.py:214
  122.4 1.1 copy-done.8
  123.6 3.6 %fusion.50 = f32[256,1536]{1,0:T(8,128)S(1)} fusion(bf16[1408,1536]{1,0:T(8,128)(2,1)} %param.32, f32[256,1408]{1,0:T(8,128)S(1)} %broadcast_divide_fusion, f32[1408]{0:T(1024)S(1)} %copy-done.16), kind=kOutput, calls=%fused_computation.77 | convolution fusion | flops 1108017152 | bytes 7345664 | tf_op jit(solution)/shard_map/dot_general | solution.py:418
  127.2 4.3 %convolution_convert_fusion.2 = bf16[256,1408]{1,0:T(8,128)(2,1)S(1)} fusion(bf16[1536,1408]{1,0:T(8,128)(2,1)} %param.33, f32[256,1536]{1,0:T(8,128)S(1)} %fusion.50), kind=kOutput, calls=%fused_computation.19 | convolution fusion | flops 1111195648 | bytes 6619136 | tf_op jit(solution)/shard_map/dot_general | solution.py:427
  131.5 7.8 %shard_map.196 = f32[64,1408]{1,0:T(8,128)S(1)} custom-call(bf16[4,64,1408]{2,1,0:T(8,128)(2,1)S(1)} %bitcast.152), custom_call_target="tpu_custom_call" | custom-call | tf_op jit(solution)/shard_map/pallas_call | solution.py:287
  140.1 8.1 %shard_map.197 = bf16[4,64,1408]{2,1,0:T(8,128)(2,1)S(1)} custom-call(bf16[64,1408]{1,0:T(8,128)(2,1)S(1)} %fusion.84.src), custom_call_target="tpu_custom_call" | custom-call | tf_op jit(solution)/shard_map/pallas_call | solution.py:214
  148.2 7.1 %convolution_convert_fusion.1 = bf16[256,1408]{1,0:T(8,128)(2,1)S(1)} fusion(bf16[1408,1536]{1,0:T(8,128)(2,1)} %param.32, f32[256,1536]{1,0:T(8,128)} %copy-done.19, bf16[256,1408]{1,0:T(8,128)(2,1)S(1)} %bitcast.150, bf16[1536,1408]{1,0:T(8,128)(2,1)} %param.33), kind=kOutput, calls=%fused_computation.18 | convolution fusion | flops 2222817280 | bytes 11665408 | tf_op jit(solution)/shard_map/rh,wh->rw/dot_general | solution.py:316
  155.3 7.9 %shard_map.198 = f32[64,1408]{1,0:T(8,128)S(1)} custom-call(bf16[4,64,1408]{2,1,0:T(8,128)(2,1)S(1)} %bitcast.151), custom_call_target="tpu_custom_call" | custom-call | tf_op jit(solution)/shard_map/pallas_call | solution.py:287
  163.2 1.1 multiply_reduce_fusion.4
  164.3 1.4 fusion.54
  165.8 5.8 %shard_map.199 = f32[4,64,256]{2,1,0:T(8,128)S(1)} custom-call(f32[64,256]{1,0:T(8,128)S(1)} %pad_maximum_fusion.2.src), custom_call_target="tpu_custom_call" | custom-call | tf_op jit(solution)/shard_map/pallas_call | solution.py:214
  171.6 1.7 scatter_custom_fusion
  173.6 2.4 fusion.85
  176.0 2.1 fusion.22
  179.6 3.0 %convert_reduce_fusion = f32[512]{0:T(512)S(1)} fusion(bf16[512,4096]{1,0:T(8,128)(2,1)} %get-tuple-element.6), kind=kLoop, calls=%fused_computation.2 | loop fusion | flops 4193792 | bytes 4196352 | tf_op jit(solution)/shard_map/reduce_sum | solution.py:410
  182.6 27.3 %all-gather.2.cloned.1.call-done = bf16[512,4096]{1,0:T(8,128)(2,1)} async-done(((bf16[128,4096]{1,0:T(8,128)(2,1)}), bf16[512,4096]{1,0:T(8,128)(2,1)}) %all-gather.2.cloned.1.call-update) | async-done | bytes 4194320 | tf_op jit(solution)/shard_map/all_gather | solution.py:407
  209.8 6.8 %convolution_multiply_fusion.1 = f32[512,512]{0,1:T(8,128)} fusion(bf16[512,4096]{1,0:T(8,128)(2,1)} %all-gather.2.cloned.1.call-done, bf16[512,4096]{1,0:T(8,128)(2,1)} %get-tuple-element.6, f32[512]{0:T(512)S(1)} %broadcast_multiply_fusion), kind=kOutput, calls=%fused_computation.44 | convolution fusion | flops 2147745792 | bytes 9439232 | tf_op jit(solution)/shard_map/tc,rc->tr/dot_general | solution.py:316
  216.6 4.2 %fusion.24 = bf16[512,512]{0,1:T(8,128)(2,1)S(1)} fusion(f32[512,512]{0,1:T(8,128)} %convolution_multiply_fusion.1, bf16[512,128]{1,0:T(8,128)(2,1)S(1)} %get-tuple-element.18, bf16[512,4096]{1,0:T(8,128)(2,1)} %get-tuple-element.6, bf16[4096,128]{1,0:T(8,128)(2,1)S(1)} %copy-done.7, f32[4096]{0:T(1024)S(1)} %bitcast.166, f32[512]{0:T(512)S(1)} %convert_reduce_fusion.1, ...), kind=kOutput, calls=%fused_computation.50 | convolution fusion | flops 606928896 | bytes 6969344 | tf_op jit(solution)/shard_map/tp,rp->tr/dot_general | solution.py:316
  220.8 1.4 fusion.31
  222.2 4.2 %fusion.26 = bf16[512,4,128]{2,0,1:T(8,128)(2,1)S(1)} fusion(f32[512,512,4]{1,0,2:T(8,128)} %copy-done.4, bf16[512,4,128]{0,2,1:T(8,128)(2,1)S(1)} %bitcast.161, f32[4,512]{1,0:T(4,128)S(1)} %fusion.31, f32[4,512]{1,0:T(4,128)S(1)} %log_add_fusion, pred[512]{0:T(512)(128)(4,1)S(1)} %iota_compare_fusion, bf16[512,768]{1,0:T(8,128)(2,1)S(1)} %bitcast.156), kind=kOutput, calls=%fused_computation.52 | convolution fusion | flops 543686656 | bytes 5521920 | tf_op jit(solution)/shard_map/hts,sd->htd/dot_general | solution.py:316
  227.0 8.3 %shard_map.200 = bf16[4,128,512]{2,1,0:T(8,128)(2,1)S(1)} custom-call(bf16[4,128,512]{2,1,0:T(8,128)(2,1)S(1)} %convert_element_type.148.src), custom_call_target="tpu_custom_call" | custom-call | tf_op jit(solution)/shard_map/pallas_call | solution.py:71
  235.6 1.0 copy.36
  (84 shorter events, 8.0 us)
Async XLA Ops:
  7.2 114.6 %copy-start = (bf16[128,1408]{1,0:T(8,128)(2,1)S(1)}, bf16[128,1408]{1,0:T(8,128)(2,1)}, u32[]{:S(2)}) copy-start(bf16[128,1408]{1,0:T(8,128)(2,1)} %param.30) | copy-start | bytes 1081348
  7.2 202.7 %all-gather.2.cloned.1.call-start = ((), (), s32[]{:S(2)}) async-start(), calls=%async_computation | async-start | bytes 5242880 | tf_op jit(solution)/shard_map/all_gather | solution.py:407
  8.4 1.9 copy-start.1
  66.3 1.9 copy-start.4
  68.2 2.3 copy-start.5
  75.0 32.0 %copy-start.11 = (bf16[1,128,4096]{2,1,0:T(8,128)(2,1)S(1)}, bf16[1,128,4096]{2,1,0:T(8,128)(2,1)}, u32[]{:S(2)}) copy-start(bf16[1,128,4096]{2,1,0:T(8,128)(2,1)} %param.18) | copy-start | bytes 3145732
  107.4 1.3 copy-start.2
  107.4 1.7 copy-start.15
  107.4 2.5 %copy-start.6 = (bf16[4096,128]{1,0:T(8,128)(2,1)S(1)}, bf16[4096,128]{1,0:T(8,128)(2,1)}, u32[]{:S(2)}) copy-start(bf16[4096,128]{1,0:T(8,128)(2,1)} %param.26) | copy-start | bytes 3145732
  107.4 2.5 %copy-start.14 = (f32[1,4096]{1,0:T(1,128)S(1)}, f32[1,4096]{1,0:T(1,128)}, u32[]{:S(2)}) copy-start(f32[1,4096]{1,0:T(1,128)} %param.23) | copy-start | bytes 49156
  107.4 4.7 %copy-start.18 = (bf16[1,128,128]{2,1,0:T(8,128)(2,1)S(1)}, bf16[1,128,128]{2,1,0:T(8,128)(2,1)}, u32[]{:S(2)}) copy-start(bf16[1,128,128]{2,1,0:T(8,128)(2,1)} %param.27) | copy-start | bytes 98308
  112.1 8.7 %copy-start.17 = (s32[1,256]{1,0:T(1,128)S(1)}, s32[1,256]{1,0:T(1,128)}, u32[]{:S(2)}) copy-start(s32[1,256]{1,0:T(1,128)} %param.29) | copy-start | bytes 3076
  121.7 1.8 copy-start.16
  122.4 1.1 copy-start.8
  127.2 4.3 %copy-start.19 = (f32[256,1536]{1,0:T(8,128)}, f32[256,1536]{1,0:T(8,128)S(1)}, u32[]{:S(2)}) copy-start(f32[256,1536]{1,0:T(8,128)S(1)} %fusion.50) | copy-start | bytes 4718596
  127.2 12.4 %copy-start.12 = (f32[1408]{0:T(1024)S(1)}, f32[1408]{0:T(1024)}, u32[]{:S(2)}) copy-start(f32[1408]{0:T(1024)} %param.34) | copy-start | bytes 16900
  127.2 12.4 %copy-start.13 = (f32[1408]{0:T(1024)S(1)}, f32[1408]{0:T(1024)}, u32[]{:S(2)}) copy-start(f32[1408]{0:T(1024)} %param.35) | copy-start | bytes 16900
  139.9 8.3 %copy-start.9 = (f32[64,1408]{1,0:T(8,128)}, f32[64,1408]{1,0:T(8,128)S(1)}, u32[]{:S(2)}) copy-start(f32[64,1408]{1,0:T(8,128)S(1)} %get-tuple-element.19) | copy-start | bytes 1081348
  148.2 16.1 %copy-start.10 = (f32[64,1408]{1,0:T(8,128)S(1)}, f32[64,1408]{1,0:T(8,128)}, u32[]{:S(2)}) copy-start(f32[64,1408]{1,0:T(8,128)} %copy-done.9) | copy-start | bytes 1081348
  164.3 9.2 %copy-start.7 = (bf16[4096,128]{1,0:T(8,128)(2,1)S(1)}, bf16[4096,128]{1,0:T(8,128)(2,1)}, u32[]{:S(2)}) copy-start(bf16[4096,128]{1,0:T(8,128)(2,1)} %param.26) | copy-start | bytes 3145732
  173.6 2.5 %copy-start.3 = (f32[128,4096]{1,0:T(8,128)S(1)}, f32[128,4096]{1,0:T(8,128)}, u32[]{:S(2)}) copy-start(f32[128,4096]{1,0:T(8,128)} %copy-done.2) | copy-start | bytes 6291460
Sparse Core Ops, SparseCore 0:
  178.3 31.5 all-gather.1

commit v2 on v1

--- a/solution.py
+++ b/solution.py
@@ -83,7 +83,33 @@
 
 
 def front_kernel(
-    n, dp_n, src, weight, dst, full, send, recv, local, up_s, up_r, dn_s, dn_r, ac_s, ac_r
+    n,
+    dp_n,
+    heads,
+    src,
+    weight,
+    live,
+    dst,
+    full,
+    attended,
+    log_total,
+    total,
+    product,
+    near,
+    paired,
+    far,
+    send,
+    recv,
+    local,
+    up_s,
+    dn_s,
+    z_r,
+    x_s,
+    x_r,
+    near_s,
+    near_r,
+    far_s,
+    far_r,
 ):
     me = lax.axis_index("ctx")
     mine = lax.axis_index("dp")
@@ -93,9 +119,17 @@
     above, below = lax.rem(mine + 2, dp_n), lax.rem(mine + dp_n - 2, dp_n)
     has_up, has_down = outer + 1 < n_out, outer >= 1
     width = weight.shape[1]
+    tokens = src.shape[1]
+    n_ctx = n // 2
+    ctx_out, core = me // 2, lax.rem(me, 2)
+    partner = ctx_out * 2 + 1 - core
+    owners = [lax.rem(ctx_out + k, n_ctx) * 2 for k in range(n_ctx)]
+
+    def columns(index):
+        return pl.ds(pl.multiple_of(index * width, width), width)
 
     def block(index):
-        return full.at[:, pl.ds(pl.multiple_of(index * width, width), width)]
+        return full.at[:, columns(index)]
 
     barrier = pltpu.get_barrier_semaphore()
     for k in range(1, n):
@@ -105,76 +139,173 @@
     for peer in (across, above, below):
         pl.semaphore_signal(barrier, inc=1, device_id={"dp": peer}, device_id_type=MESH)
     pl.semaphore_wait(barrier, n + 2)
+
+    side = jnp.minimum(outer, n_out - 1 - outer)
+    origins = [outer]
+    for j in range(1, n_out):
+        paired_step = (j + 1) // 2
+        near_origin = outer - paired_step if j % 2 == 1 else outer + paired_step
+        far_origin = jnp.where(outer > n_out - 1 - outer, outer - (j - side), outer + (j - side))
+        origins.append(jnp.where(j <= 2 * side, near_origin, far_origin))
+
+    def up(j):
+        at = origins[j]
+        source = weight if j == 0 else block(at * 2 + inner)
+        return remote(source, block(at * 2 + inner), up_s.at[at], z_r.at[at], "dp", above)
+
+    def down(j):
+        at = origins[j]
+        source = weight if j == 0 else block(at * 2 + inner)
+        return remote(source, block(at * 2 + inner), dn_s.at[at], z_r.at[at], "dp", below)
+
+    def cross(j):
+        at = origins[j]
+        source = weight if j == 0 else block(at * 2 + inner)
+        return remote(source, block(at * 2 + inner), x_s.at[at], x_r.at[at], "dp", across)
+
+    def goes_up(j):
+        return has_up if j == 0 else jnp.logical_and(has_up, origins[j] < outer)
+
+    def goes_down(j):
+        return has_down if j == 0 else jnp.logical_and(has_down, origins[j] > outer)
+
+    own_weight = pltpu.make_async_copy(weight, block(mine), local.at[1])
+
+    def acquire(kind, j):
+        if kind == "x":
+            cross(j).wait_recv()
+            return origins[j] * 2 + 1 - inner
+        if j:
+            up(j).wait_recv()
+        pl.when(goes_up(j))(lambda: up(j).start())
+        pl.when(goes_down(j))(lambda: down(j).start())
+        cross(j).start()
+        if j == 0:
+            own_weight.start()
+            own_weight.wait()
+        return origins[j] * 2 + inner
+
     copies = swap_start(n, src, dst, send, recv)
-
-    def up(source, index, step):
-        return remote(source, block(index), up_s.at[step], up_r.at[step], "dp", above)
-
-    def down(source, index, step):
-        return remote(source, block(index), dn_s.at[step], dn_r.at[step], "dp", below)
-
-    def cross(source, index, step):
-        return remote(source, block(index), ac_s.at[step], ac_r.at[step], "dp", across)
-
-    pl.when(has_up)(lambda: up(weight, mine, 0).start())
-    pl.when(has_down)(lambda: down(weight, mine, 0).start())
-    cross(weight, mine, 0).start()
     own = pltpu.make_async_copy(src.at[me], dst.at[me], local.at[0])
     own.start()
-    own_weight = pltpu.make_async_copy(weight, block(mine), local.at[1])
-    own_weight.start()
-    for step in range(1, n_out):
-        low, high = mine - 2 * step, mine + 2 * step
-
-        @pl.when(outer >= step)
-        def _():
-            up(block(low), low, step - 1).wait_recv()
-            pl.when(has_up)(lambda: up(block(low), low, step).start())
-            cross(block(low), low, step).start()
-
-        @pl.when(outer + step < n_out)
-        def _():
-            down(block(high), high, step - 1).wait_recv()
-            pl.when(has_down)(lambda: down(block(high), high, step).start())
-            cross(block(high), high, n_out + step).start()
-
+    slots = [("z", 0)]
+    for j in range(1, n_out):
+        slots += [("z", j), ("x", j - 1)]
+    slots.append(("x", n_out - 1))
+    positions = [acquire(*slots[0])]
     own.wait()
-    own_weight.wait()
     for copy in copies:
         copy.wait()
-    pl.when(has_up)(lambda: up(weight, mine, 0).wait_send())
-    pl.when(has_down)(lambda: down(weight, mine, 0).wait_send())
-    cross(weight, mine, 0).wait()
-    for step in range(1, n_out):
-        low, high = mine - 2 * step, mine + 2 * step
-
-        @pl.when(outer >= step)
-        def _():
-            pl.when(has_up)(lambda: up(block(low), low, step).wait_send())
-            cross(block(low), low, step).wait()
-
-        @pl.when(outer + step < n_out)
-        def _():
-            pl.when(has_down)(lambda: down(block(high), high, step).wait_send())
-            cross(block(high), high, n_out + step).wait()
-
-
-def front(pieces, weight, n, dp_n, collective_id):
+
+    sequence = n * tokens
+    keys = dst[:, :, heads * HEAD : (heads + 1) * HEAD].reshape(sequence, HEAD)
+    values = dst[:, :, (heads + 1) * HEAD :].reshape(sequence, HEAD)
+    is_live = live[...] > 0.5
+    group = min(n, 4)
+    pieces = [(h, r) for h in range(heads) for r in range(0, n, group)]
+    for step, (h, r) in enumerate(pieces):
+        at = slice(r * tokens, (r + group) * tokens)
+        queries = dst[r : r + group, :, h * HEAD : (h + 1) * HEAD].reshape(group * tokens, HEAD)
+        scores = lax.dot_general(
+            queries, keys, (((1,), (1,)), ((), ())), preferred_element_type=jnp.float32
+        ) / math.sqrt(HEAD)
+        scores = jnp.where(is_live, scores, MASKED)
+        highest = jnp.max(scores, axis=-1, keepdims=True)
+        weights_rows = jnp.exp(scores - highest)
+        denominator = jnp.sum(weights_rows, axis=-1, keepdims=True)
+        numerator = jnp.dot(
+            weights_rows.astype(jnp.bfloat16), values, preferred_element_type=jnp.float32
+        )
+        attended[at, h * HEAD : (h + 1) * HEAD] = (numerator / denominator).astype(jnp.bfloat16)
+        log_total[at, h : h + 1] = highest + jnp.log(denominator)
+        if step == len(pieces) // 2 - 1:
+            positions.append(acquire(*slots[1]))
+
+    def near_copy(t, k):
+        source = product.at[t, owners[k] + 1 - core]
+        return remote(source, near.at[t, k], near_s.at[t, k], near_r.at[t, k], "ctx", partner)
+
+    def far_copy(t, k):
+        return remote(
+            paired.at[t, k - 1],
+            far.at[t, k - 1],
+            far_s.at[t, k - 1],
+            far_r.at[t, k - 1],
+            "ctx",
+            owners[k] + core,
+        )
+
+    def pair(t):
+        for k in range(1, n_ctx):
+            near_copy(t, k).wait_recv()
+            paired[t, k - 1] = (
+                product[t, owners[k] + core].astype(jnp.float32) + near[t, k].astype(jnp.float32)
+            ).astype(jnp.bfloat16)
+            far_copy(t, k).start()
+
+    for t, slot in enumerate(slots):
+        if t >= len(positions):
+            positions.append(acquire(*slot))
+        part = jnp.dot(
+            attended[...], full[:, columns(positions[t])], preferred_element_type=jnp.float32
+        )
+        product[t] = part.astype(jnp.bfloat16).reshape(n, tokens, width)
+        for k in list(range(1, n_ctx)) + [0]:
+            near_copy(t, k).start()
+        if t:
+            pair(t - 1)
+    pair(len(slots) - 1)
+    for t in range(len(slots)):
+        near_copy(t, 0).wait_recv()
+        whole = product[t, me].astype(jnp.float32) + near[t, 0].astype(jnp.float32)
+        for k in range(1, n_ctx):
+            far_copy(t, k).wait_recv()
+            whole = whole + far[t, k - 1].astype(jnp.float32)
+        total[:, columns(positions[t])] = whole
+
+    for j in range(n_out):
+        pl.when(goes_up(j))(lambda: up(j).wait_send())
+        pl.when(goes_down(j))(lambda: down(j).wait_send())
+        cross(j).wait_send()
+    for t in range(len(slots)):
+        for k in range(n_ctx):
+            near_copy(t, k).wait_send()
+        for k in range(1, n_ctx):
+            far_copy(t, k).wait_send()
+
+
+def front(pieces, weight, live, n, dp_n, heads, collective_id):
     dma = pltpu.SemaphoreType.DMA
-    n_out = dp_n // 2
+    n_out, n_ctx = dp_n // 2, n // 2
+    tokens = pieces.shape[1]
+    rows, width = weight.shape
+    part = (tokens, width)
+    half = jnp.bfloat16
     return pl.pallas_call(
-        functools.partial(front_kernel, n, dp_n),
+        functools.partial(front_kernel, n, dp_n, heads),
         out_shape=(
             jax.ShapeDtypeStruct(pieces.shape, pieces.dtype),
-            jax.ShapeDtypeStruct((weight.shape[0], weight.shape[1] * dp_n), weight.dtype),
+            jax.ShapeDtypeStruct((rows, width * dp_n), weight.dtype),
+            jax.ShapeDtypeStruct((n * tokens, heads * HEAD), half),
+            jax.ShapeDtypeStruct((n * tokens, heads), jnp.float32),
+            jax.ShapeDtypeStruct((tokens, width * dp_n), jnp.float32),
         ),
-        in_specs=[VMEM_SPEC] * 2,
-        out_specs=(VMEM_SPEC, VMEM_SPEC),
-        scratch_shapes=[dma((n - 1,)), dma((n - 1,)), dma((2,))]
-        + [dma((n_out,))] * 4
-        + [dma((2 * n_out,))] * 2,
+        in_specs=[VMEM_SPEC] * 3,
+        out_specs=(VMEM_SPEC,) * 5,
+        scratch_shapes=[
+            pltpu.VMEM((dp_n, n) + part, half),
+            pltpu.VMEM((dp_n, n_ctx) + part, half),
+            pltpu.VMEM((dp_n, n_ctx - 1) + part, half),
+            pltpu.VMEM((dp_n, n_ctx - 1) + part, half),
+            dma((n - 1,)),
+            dma((n - 1,)),
+            dma((2,)),
+        ]
+        + [dma((n_out,))] * 5
+        + [dma((dp_n, n_ctx))] * 2
+        + [dma((dp_n, n_ctx - 1))] * 2,
         compiler_params=params(collective_id),
-    )(pieces, weight)
+    )(pieces, weight, live)
 
 
 def collect_kernel(n, src, dst, send, recv, local):
@@ -360,25 +491,16 @@
             for c in range(n)
         ]
     )
-    swapped, weight = front(pieces, out_weight, n, dp_n, 0)
+    is_live = jnp.arange(sequence, dtype=jnp.int32) < clip_length
+    swapped, weight, attended, log_total, product = front(
+        pieces, out_weight, is_live.astype(jnp.float32)[None], n, dp_n, heads, 0
+    )
     swapped = swapped.reshape(sequence, (heads + 2) * HEAD)
     query_heads = swapped[:, : heads * HEAD].reshape(sequence, heads, HEAD)
     key_rows = swapped[:, heads * HEAD : (heads + 1) * HEAD]
     value_rows = swapped[:, (heads + 1) * HEAD :]
 
-    is_live = jnp.arange(sequence, dtype=jnp.int32) < clip_length
-    scores = matmul("thd,sd->hts", query_heads, key_rows) / math.sqrt(HEAD)
-    scores = jnp.where(is_live, scores, MASKED)
-    highest = jnp.max(scores, axis=-1)
-    weights_rows = jnp.exp(scores - highest[..., None])
-    denominator = jnp.sum(weights_rows, axis=-1)
-    numerator = matmul("hts,sd->htd", weights_rows.astype(jnp.bfloat16), value_rows)
-    attended_heads = (numerator / denominator[..., None]).astype(jnp.bfloat16)
-    attended = jnp.transpose(attended_heads, (1, 0, 2)).reshape(sequence, heads * HEAD)
-    log_total = highest + jnp.log(denominator)
-
-    product = matmul("tr,rc->tc", attended, weight).astype(jnp.bfloat16)
-    residual = stream[0].astype(jnp.float32) + reduce(product.reshape(n, tokens, width), n, 1)
+    residual = stream[0].astype(jnp.float32) + product
     centred = residual - jnp.mean(residual, axis=-1, keepdims=True)
     inverse = lax.rsqrt(jnp.mean(centred * centred, axis=-1, keepdims=True) + EPSILON)
     unit_rows = centred * inverse
@@ -404,7 +526,7 @@
     )
     bundles = collect(bundle, n, 2).reshape(sequence, 3 * PATCH)
     gathered = bundles[:, :PATCH]
-    unit_full = lax.all_gather(unit_rows.astype(jnp.bfloat16), "ctx", axis=0, tiled=True)
+    unit_full = collect(unit_rows.astype(jnp.bfloat16), n, 1).reshape(sequence, width)
     unit_out = matmul("tc,rc->tr", unit_full, weight)
     gained_out = matmul("rc,cp->rp", weight, gained.astype(jnp.bfloat16)).astype(jnp.bfloat16)
     weight_sum = jnp.sum(weight.astype(jnp.float32), axis=-1)
@@ -485,13 +607,13 @@
     ).astype(jnp.bfloat16)
     slope_heads = attended_slope.reshape(sequence, heads, HEAD)
     row_delta = jnp.sum(
-        jnp.transpose(slope_heads, (1, 0, 2)).astype(jnp.float32)
-        * attended_heads.astype(jnp.float32),
+        slope_heads.astype(jnp.float32)
+        * attended.reshape(sequence, heads, HEAD).astype(jnp.float32),
         axis=-1,
-    )
+    ).T
     back_scores = matmul("thd,sd->hts", query_heads, key_rows) / math.sqrt(HEAD)
     back_scores = jnp.where(is_live, back_scores, MASKED)
-    back_weights = jnp.exp(back_scores - log_total[..., None])
+    back_weights = jnp.exp(back_scores - log_total.T[..., None])
     slopes = matmul("thd,sd->hts", slope_heads, value_rows)
     score_slope = (back_weights * (slopes - row_delta[..., None])).astype(jnp.bfloat16)
     query_slope = matmul("hts,sd->htd", score_slope, key_rows) / math.sqrt(HEAD)

time: 245 us -> 206 us (0.84)
  waiting for transfers between devices: 27.3 us -> 0 us
  between operations: 17.9 us -> 4.58 us
  Pallas kernels: 131 us -> 141 us
  matrix products: 44.1 us -> 36.2 us
  other arithmetic: 15.1 us -> 11.6 us
  local copies, waits for them, and re-layouts: 9.56 us -> 12.1 us
    pallas_call x3 -> x2, Pallas kernels: 47.7 us -> 15.8 us  [reduce(): pl.pallas_call(functools.partial(reduce_kernel, n), out_shape=jax.ShapeDt...]
    pallas_call x3 -> x4, Pallas kernels: 20.3 us -> 48.3 us  [collect(): pl.pallas_call(functools.partial(collect_kernel, n), out_shape=jax.ShapeD...]
    all_gather x1 -> x0, waiting for transfers between devices: 27.3 us -> none  [per_device(): lax.all_gather(unit_rows.astype(jnp.bfloat16), 'ctx', axis=0, tiled=True)]
    pallas_call x1, Pallas kernels: 54.3 us -> 68.7 us  [front(): pl.pallas_call(functools.partial(front_kernel, n, dp_n, heads), out_shape...]
    dot_general x9 -> x7, matrix products: 33.5 us -> 26 us  [matmul(): jnp.einsum(subscripts, left, right, preferred_element_type=jnp.float32)]
  transfers between devices with their start and end apart: 1 -> 0, of which waited for: 1 -> 0; matrix products, arithmetic and copies ran while one was open for 2% -> 0% of each run, Pallas kernels for 0% -> 0%
where the time goes in v2:
time: 206 us; the launch traced here: 205 us
  Pallas kernels  141 us (68%)
  matrix products  36.2 us (18%)
  local copies, waits for them, and re-layouts  12.1 us (6%)
  other arithmetic  11.6 us (6%)
  between operations  4.58 us (2%)
    pallas_call x1, Pallas kernels, front(): pl.pallas_call(functools.partial(front_kernel, n, dp_n, heads), out_shape...  68.7 us
    pallas_call x4, Pallas kernels, collect(): pl.pallas_call(functools.partial(collect_kernel, n), out_shape=jax.ShapeD...  48.3 us
    dot_general x7, matrix products, matmul(): jnp.einsum(subscripts, left, right, preferred_element_type=jnp.float32)  26 us
    pallas_call x2, Pallas kernels, reduce(): pl.pallas_call(functools.partial(reduce_kernel, n), out_shape=jax.ShapeDt...  15.8 us
    pallas_call x1, Pallas kernels, swap(): pl.pallas_call(functools.partial(swap_kernel, n), out_shape=jax.ShapeDtyp...  8.17 us
    unnamed x49, local copies, waits for them, and re-layouts  4.32 us
    dot_general x1, matrix products, per_device(): down_part = jnp.dot(active, down_weight, preferred_element_type=jnp.float32)  4.29 us

profile of v2, /device:TPU:1, one launch (start us, length us, event | category | flops | bytes accessed | tf_op | source)
XLA Modules:
  0.0 205.3 jit_solution(4658599680977675601)
XLA Ops:
  0.6 1.2 slice_bitcast_fusion.7
  1.8 0.9 slice_bitcast_fusion.17
  2.7 0.8 slice_bitcast_fusion.16
  4.5 68.7 %shard_map.193 = (bf16[4,128,768]{2,1,0:T(8,128)(2,1)S(1)}, bf16[512,4096]{1,0:T(8,128)(2,1)}, bf16[512,512]{1,0:T(8,128)(2,1)S(1)}, f32[512,4]{1,0:T(8,128)S(1)}, f32[128,4096]{1,0:T(8,128)S(1)}) custom-call(bf16[4,128,768]{2,1,0:T(8,128)(2,1)S(1)} %pad_maximum_fusion.src, bf16[512,512]{1,0:T(8,128)(2,1)S(1)} %copy-done.1, ...), custom_call_target="tpu_custom_call" | custom-call | tf_op jit(solution)/shard_map/pallas_call | solution.py:284
  74.8 1.3 copy-done.8
  76.1 2.1 %fusion.3 = (f32[128]{0:T(128)S(1)}, f32[128]{0:T(128)S(1)}) fusion(bf16[4096,128]{1,0:T(8,128)(2,1)S(1)} %copy-done.8, f32[4096]{0:T(1024)S(1)} %bitcast.137, f32[4096]{0:T(1024)S(1)} %bitcast.141), kind=kLoop, calls=%fused_computation.13 | loop fusion | flops 2621184 | bytes 1082368 | tf_op jit(solution)/shard_map/reduce_sum | solution.py:517
  79.0 1.8 fusion.52
  81.0 6.7 %shard_map.194 = bf16[4,128,384]{2,1,0:T(8,128)(2,1)S(1)} custom-call(bf16[128,384]{1,0:T(8,128)(2,1)S(1)} %pad_maximum_fusion.1.src), custom_call_target="tpu_custom_call" | custom-call | tf_op jit(solution)/shard_map/pallas_call | solution.py:345
  87.7 0.9 gather_fusion
  89.3 1.2 copy-done.11
  90.5 3.6 %fusion.42 = f32[256,1536]{1,0:T(8,128)S(1)} fusion(bf16[1408,1536]{1,0:T(8,128)(2,1)} %param.32, f32[256,1408]{1,0:T(8,128)S(1)} %broadcast_divide_fusion, f32[1408]{0:T(1024)S(1)} %copy-done.20), kind=kOutput, calls=%fused_computation.64 | convolution fusion | flops 1108017152 | bytes 7345664 | tf_op jit(solution)/shard_map/dot_general | solution.py:540
  94.1 4.3 %convolution_convert_fusion.1 = bf16[256,1408]{1,0:T(8,128)(2,1)S(1)} fusion(bf16[1536,1408]{1,0:T(8,128)(2,1)} %param.33, f32[256,1536]{1,0:T(8,128)S(1)} %fusion.42), kind=kOutput, calls=%fused_computation.12 | convolution fusion | flops 1111195648 | bytes 6619136 | tf_op jit(solution)/shard_map/dot_general | solution.py:549
  98.4 7.9 %shard_map.195 = f32[64,1408]{1,0:T(8,128)S(1)} custom-call(bf16[4,64,1408]{2,1,0:T(8,128)(2,1)S(1)} %bitcast.127), custom_call_target="tpu_custom_call" | custom-call | tf_op jit(solution)/shard_map/pallas_call | solution.py:418
  106.9 8.0 %shard_map.196 = bf16[4,64,1408]{2,1,0:T(8,128)(2,1)S(1)} custom-call(bf16[64,1408]{1,0:T(8,128)(2,1)S(1)} %fusion.74.src), custom_call_target="tpu_custom_call" | custom-call | tf_op jit(solution)/shard_map/pallas_call | solution.py:345
  115.0 7.1 %convolution_convert_fusion = bf16[256,1408]{1,0:T(8,128)(2,1)S(1)} fusion(bf16[1408,1536]{1,0:T(8,128)(2,1)} %param.32, f32[256,1536]{1,0:T(8,128)} %copy-done.23, bf16[256,1408]{1,0:T(8,128)(2,1)S(1)} %bitcast.125, bf16[1536,1408]{1,0:T(8,128)(2,1)} %param.33), kind=kOutput, calls=%fused_computation.11 | convolution fusion | flops 2222817280 | bytes 11665408 | tf_op jit(solution)/shard_map/rh,wh->rw/dot_general | solution.py:447
  122.1 7.9 %shard_map.197 = f32[64,1408]{1,0:T(8,128)S(1)} custom-call(bf16[4,64,1408]{2,1,0:T(8,128)(2,1)S(1)} %bitcast.126), custom_call_target="tpu_custom_call" | custom-call | tf_op jit(solution)/shard_map/pallas_call | solution.py:418
  129.9 1.1 multiply_reduce_fusion.5
  131.2 1.4 fusion.46
  132.6 5.8 %shard_map.198 = f32[4,64,256]{2,1,0:T(8,128)S(1)} custom-call(f32[64,256]{1,0:T(8,128)S(1)} %pad_maximum_fusion.2.src), custom_call_target="tpu_custom_call" | custom-call | tf_op jit(solution)/shard_map/pallas_call | solution.py:345
  138.4 1.5 scatter_custom_fusion
  140.2 2.4 %fusion.75 = (f32[128]{0:T(128)S(1)}, f32[128]{0:T(128)S(1)}, f32[128,4096]{1,0:T(8,128)S(1)}) fusion(f32[128]{0:T(128)S(1)} %get-tuple-element.50, f32[128,4096]{1,0:T(8,128)} %copy-done.6, f32[128]{0:T(128)S(1)} %broadcast_multiply_fusion.6, f32[4096]{0:T(1024)S(1)} %bitcast.139, bf16[4096,128]{1,0:T(8,128)(2,1)S(1)} %copy-done.9, ...), kind=kOutput, calls=%fused_computation.151 | convolution fusion | flops 137363200 | bytes 5294084 | tf_op jit(solution)/shard_map/tp,dp->td/dot_general | solution.py:447
  142.7 1.8 fusion.16
  144.4 27.8 %shard_map.199 = bf16[4,128,4096]{2,1,0:T(8,128)(2,1)S(1)} custom-call(bf16[128,4096]{1,0:T(8,128)(2,1)S(1)} %get-tuple-element.34.src), custom_call_target="tpu_custom_call" | custom-call | tf_op jit(solution)/shard_map/pallas_call | solution.py:345
  172.3 3.3 %convolution_multiply_fusion.1 = f32[512,512]{0,1:T(8,128)} fusion(bf16[512,4096]{1,0:T(8,128)(2,1)S(1)} %bitcast.118, bf16[512,4096]{1,0:T(8,128)(2,1)S(1)} %copy-done.10, f32[512]{0:T(512)S(1)} %broadcast_multiply_fusion), kind=kOutput, calls=%fused_computation.35 | convolution fusion | flops 2147745792 | bytes 9439232 | tf_op jit(solution)/shard_map/tc,rc->tr/dot_general | solution.py:447
  176.4 5.0 %fusion.18 = bf16[512,512]{0,1:T(8,128)(2,1)} fusion(f32[512,512]{0,1:T(8,128)} %convolution_multiply_fusion.1, bf16[512,128]{1,0:T(8,128)(2,1)S(1)} %get-tuple-element.30, bf16[512,4096]{1,0:T(8,128)(2,1)} %get-tuple-element.11, bf16[4096,128]{1,0:T(8,128)(2,1)S(1)} %copy-done.9, f32[4096]{0:T(1024)S(1)} %bitcast.140, f32[512]{0:T(512)S(1)} %convert_reduce_fusion.1, ...), kind=kOutput, calls=%fused_computation.41 | convolution fusion | flops 606928896 | bytes 6969344 | tf_op jit(solution)/shard_map/tp,rp->tr/dot_general | solution.py:447
  181.4 2.1 %copy.49 = bf16[512,4,128]{2,1,0:T(4,128)(2,1)} copy(bf16[512,4,128]{0,2,1:T(8,128)(2,1)} %bitcast.135) | data formatting | bytes 1048576 | tf_op jit(solution)/shard_map/reshape | solution.py:608
  183.8 1.7 multiply_reduce_fusion.3
  185.9 2.6 %fusion.50 = f32[512,512,4]{1,0,2:T(8,128)} fusion(bf16[512,4,128]{0,2,1:T(8,128)(2,1)S(1)} %bitcast.132, bf16[512,768]{1,0:T(8,128)(2,1)S(1)} %bitcast.129), kind=kOutput, calls=%fused_computation.96 | convolution fusion | flops 268435456 | bytes 4849664 | tf_op jit(solution)/shard_map/thd,sd->hts/dot_general | solution.py:447
  188.7 4.2 %fusion.20 = bf16[512,4,128]{2,0,1:T(8,128)(2,1)S(1)} fusion(f32[512,512,4]{1,0,2:T(8,128)} %fusion.50, bf16[512,4,128]{0,2,1:T(8,128)(2,1)S(1)} %bitcast.136, f32[4,512]{1,0:T(4,128)S(1)} %copy.50, f32[4,512]{1,0:T(4,128)S(1)} %copy.47, pred[512]{0:T(512)(128)(4,1)S(1)} %iota_compare_fusion, bf16[512,768]{1,0:T(8,128)(2,1)S(1)} %bitcast.130), kind=kOutput, calls=%fused_computation.43 | convolution fusion | flops 543686656 | bytes 5521920 | tf_op jit(solution)/shard_map/hts,sd->htd/dot_general | solution.py:447
  193.5 8.2 %shard_map.200 = bf16[4,128,512]{2,1,0:T(8,128)(2,1)S(1)} custom-call(bf16[4,128,512]{2,1,0:T(8,128)(2,1)S(1)} %convert_element_type.143.src), custom_call_target="tpu_custom_call" | custom-call | tf_op jit(solution)/shard_map/pallas_call | solution.py:71
  201.9 1.0 copy.54
  202.9 0.6 slice_reduce_fusion
  (90 shorter events, 6.0 us)
Async XLA Ops:
  0.6 87.9 %copy-start = (bf16[128,1408]{1,0:T(8,128)(2,1)S(1)}, bf16[128,1408]{1,0:T(8,128)(2,1)}, u32[]{:S(2)}) copy-start(bf16[128,1408]{1,0:T(8,128)(2,1)} %param.30) | copy-start | bytes 1081348
  1.8 2.7 %copy-start.1 = (bf16[512,512]{1,0:T(8,128)(2,1)S(1)}, bf16[512,512]{1,0:T(8,128)(2,1)}, u32[]{:S(2)}) copy-start(bf16[512,512]{1,0:T(8,128)(2,1)} %weight.1) | copy-start | bytes 1572868
  3.6 69.7 %copy-start.14 = (bf16[1,128,4096]{2,1,0:T(8,128)(2,1)S(1)}, bf16[1,128,4096]{2,1,0:T(8,128)(2,1)}, u32[]{:S(2)}) copy-start(bf16[1,128,4096]{2,1,0:T(8,128)(2,1)} %param.18) | copy-start | bytes 3145732
  73.2 0.8 copy-start.2
  73.2 0.9 copy-start.4
  74.1 6.7 %copy-start.6 = (f32[128,4096]{1,0:T(8,128)}, f32[128,4096]{1,0:T(8,128)S(1)}, u32[]{:S(2)}) copy-start(f32[128,4096]{1,0:T(8,128)S(1)} %get-tuple-element.33) | copy-start | bytes 6291460
  74.1 0.7 copy-start.19
  74.1 2.0 copy-start.8
  74.1 2.0 copy-start.18
  74.1 4.9 %copy-start.22 = (bf16[1,128,128]{2,1,0:T(8,128)(2,1)S(1)}, bf16[1,128,128]{2,1,0:T(8,128)(2,1)}, u32[]{:S(2)}) copy-start(bf16[1,128,128]{2,1,0:T(8,128)(2,1)} %param.27) | copy-start | bytes 98308
  79.0 8.6 %copy-start.21 = (s32[1,256]{1,0:T(1,128)S(1)}, s32[1,256]{1,0:T(1,128)}, u32[]{:S(2)}) copy-start(s32[1,256]{1,0:T(1,128)} %param.29) | copy-start | bytes 3076
  88.6 1.9 copy-start.20
  89.3 1.2 copy-start.11
  94.1 4.3 %copy-start.23 = (f32[256,1536]{1,0:T(8,128)}, f32[256,1536]{1,0:T(8,128)S(1)}, u32[]{:S(2)}) copy-start(f32[256,1536]{1,0:T(8,128)S(1)} %fusion.42) | copy-start | bytes 4718596
  94.1 12.4 %copy-start.16 = (f32[1408]{0:T(1024)S(1)}, f32[1408]{0:T(1024)}, u32[]{:S(2)}) copy-start(f32[1408]{0:T(1024)} %param.34) | copy-start | bytes 16900
  94.1 12.4 %copy-start.17 = (f32[1408]{0:T(1024)S(1)}, f32[1408]{0:T(1024)}, u32[]{:S(2)}) copy-start(f32[1408]{0:T(1024)} %param.35) | copy-start | bytes 16900
  106.8 8.1 %copy-start.12 = (f32[64,1408]{1,0:T(8,128)}, f32[64,1408]{1,0:T(8,128)S(1)}, u32[]{:S(2)}) copy-start(f32[64,1408]{1,0:T(8,128)S(1)} %get-tuple-element.31) | copy-start | bytes 1081348
  115.0 16.2 %copy-start.13 = (f32[64,1408]{1,0:T(8,128)S(1)}, f32[64,1408]{1,0:T(8,128)}, u32[]{:S(2)}) copy-start(f32[64,1408]{1,0:T(8,128)} %copy-done.12) | copy-start | bytes 1081348
  131.2 9.0 %copy-start.9 = (bf16[4096,128]{1,0:T(8,128)(2,1)S(1)}, bf16[4096,128]{1,0:T(8,128)(2,1)}, u32[]{:S(2)}) copy-start(bf16[4096,128]{1,0:T(8,128)(2,1)} %param.26) | copy-start | bytes 3145732
  140.2 2.5 %copy-start.7 = (f32[128,4096]{1,0:T(8,128)S(1)}, f32[128,4096]{1,0:T(8,128)}, u32[]{:S(2)}) copy-start(f32[128,4096]{1,0:T(8,128)} %copy-done.6) | copy-start | bytes 6291460
  144.4 27.8 %copy-start.10 = (bf16[512,4096]{1,0:T(8,128)(2,1)S(1)}, bf16[512,4096]{1,0:T(8,128)(2,1)}, u32[]{:S(2)}) copy-start(bf16[512,4096]{1,0:T(8,128)(2,1)} %get-tuple-element.11) | copy-start | bytes 12582916
  176.3 7.2 %copy-start.3 = (bf16[512,512]{1,0:T(8,128)(2,1)S(1)}, bf16[512,512]{1,0:T(8,128)(2,1)}, u32[]{:S(2)}) copy-start(bf16[512,512]{1,0:T(8,128)(2,1)} %copy-done.2) | copy-start | bytes 1572868
  185.9 2.6 %copy-start.5 = (f32[512,4]{1,0:T(8,128)S(1)}, f32[512,4]{1,0:T(8,128)}, u32[]{:S(2)}) copy-start(f32[512,4]{1,0:T(8,128)} %copy-done.4) | copy-start | bytes 24580
  185.9 2.8 %copy-start.15 = (bf16[512,512]{0,1:T(8,128)(2,1)S(1)}, bf16[512,512]{0,1:T(8,128)(2,1)}, u32[]{:S(2)}) copy-start(bf16[512,512]{0,1:T(8,128)(2,1)} %fusion.18) | copy-start | bytes 1572868

commit v3 on v2

--- a/solution.py
+++ b/solution.py
@@ -37,6 +37,9 @@
     for peer in peers:
         pl.semaphore_signal(barrier, inc=1, device_id={axis: peer}, device_id_type=MESH)
     pl.semaphore_wait(barrier, len(peers))
+
+
+COST = pl.CostEstimate(flops=0, bytes_accessed=24_000_000, transcendentals=0)
 
 
 def params(collective_id):
@@ -78,6 +81,7 @@
             pltpu.SemaphoreType.DMA((n - 1,)),
             pltpu.SemaphoreType.DMA,
         ],
+        cost_estimate=COST,
         compiler_params=params(collective_id),
     )(pieces)
 
@@ -86,7 +90,9 @@
     n,
     dp_n,
     heads,
-    src,
+    query_src,
+    key_src,
+    value_src,
     weight,
     live,
     dst,
@@ -119,7 +125,7 @@
     above, below = lax.rem(mine + 2, dp_n), lax.rem(mine + dp_n - 2, dp_n)
     has_up, has_down = outer + 1 < n_out, outer >= 1
     width = weight.shape[1]
-    tokens = src.shape[1]
+    tokens = query_src.shape[0]
     n_ctx = n // 2
     ctx_out, core = me // 2, lax.rem(me, 2)
     partner = ctx_out * 2 + 1 - core
@@ -185,16 +191,35 @@
             own_weight.wait()
         return origins[j] * 2 + inner
 
-    copies = swap_start(n, src, dst, send, recv)
-    own = pltpu.make_async_copy(src.at[me], dst.at[me], local.at[0])
-    own.start()
+    span = heads * HEAD
+    per_group = HEADS // KV_HEADS
+
+    def parts(owner):
+        at = pl.ds(pl.multiple_of(owner * span, HEAD), span)
+        head = pl.ds(pl.multiple_of(((owner * heads) // per_group) * HEAD, HEAD), HEAD)
+        return [
+            (query_src.at[:, at], dst.at[me, :, pl.ds(0, span)]),
+            (key_src.at[:, head], dst.at[me, :, pl.ds(span, HEAD)]),
+            (value_src.at[:, head], dst.at[me, :, pl.ds(span + HEAD, HEAD)]),
+        ]
+
+    copies = []
+    for k in range(1, n):
+        peer = lax.rem(me + k, n)
+        for i, (source, target) in enumerate(parts(peer)):
+            copy = remote(source, target, send.at[k - 1, i], recv.at[k - 1, i], "ctx", peer)
+            copy.start()
+            copies.append(copy)
+    owns = []
+    for i, (source, target) in enumerate(parts(me)):
+        owns.append(pltpu.make_async_copy(source, target, local.at[2 + i]))
+        owns[-1].start()
     slots = [("z", 0)]
     for j in range(1, n_out):
         slots += [("z", j), ("x", j - 1)]
     slots.append(("x", n_out - 1))
     positions = [acquire(*slots[0])]
-    own.wait()
-    for copy in copies:
+    for copy in owns + copies:
         copy.wait()
 
     sequence = n * tokens
@@ -274,38 +299,39 @@
             far_copy(t, k).wait_send()
 
 
-def front(pieces, weight, live, n, dp_n, heads, collective_id):
+def front(queries, keys, values, weight, live, n, dp_n, heads, collective_id):
     dma = pltpu.SemaphoreType.DMA
     n_out, n_ctx = dp_n // 2, n // 2
-    tokens = pieces.shape[1]
+    tokens = queries.shape[0]
     rows, width = weight.shape
     part = (tokens, width)
     half = jnp.bfloat16
     return pl.pallas_call(
         functools.partial(front_kernel, n, dp_n, heads),
         out_shape=(
-            jax.ShapeDtypeStruct(pieces.shape, pieces.dtype),
+            jax.ShapeDtypeStruct((n, tokens, (heads + 2) * HEAD), half),
             jax.ShapeDtypeStruct((rows, width * dp_n), weight.dtype),
             jax.ShapeDtypeStruct((n * tokens, heads * HEAD), half),
             jax.ShapeDtypeStruct((n * tokens, heads), jnp.float32),
             jax.ShapeDtypeStruct((tokens, width * dp_n), jnp.float32),
         ),
-        in_specs=[VMEM_SPEC] * 3,
+        in_specs=[pl.BlockSpec(memory_space=pl.ANY)] * 3 + [VMEM_SPEC] * 2,
         out_specs=(VMEM_SPEC,) * 5,
         scratch_shapes=[
             pltpu.VMEM((dp_n, n) + part, half),
             pltpu.VMEM((dp_n, n_ctx) + part, half),
             pltpu.VMEM((dp_n, n_ctx - 1) + part, half),
             pltpu.VMEM((dp_n, n_ctx - 1) + part, half),
-            dma((n - 1,)),
-            dma((n - 1,)),
-            dma((2,)),
+            dma((n - 1, 3)),
+            dma((n - 1, 3)),
+            dma((5,)),
         ]
         + [dma((n_out,))] * 5
         + [dma((dp_n, n_ctx))] * 2
         + [dma((dp_n, n_ctx - 1))] * 2,
+        cost_estimate=COST,
         compiler_params=params(collective_id),
-    )(pieces, weight, live)
+    )(queries, keys, values, weight, live)
 
 
 def collect_kernel(n, src, dst, send, recv, local):
@@ -352,6 +378,7 @@
             pltpu.SemaphoreType.DMA((n,)),
             pltpu.SemaphoreType.DMA,
         ],
+        cost_estimate=COST,
         compiler_params=params(collective_id),
     )(piece)
 
@@ -429,6 +456,7 @@
             dma((n_out - 1,)),
             dma((n_out - 1,)),
         ],
+        cost_estimate=COST,
         compiler_params=params(collective_id),
     )(pieces)
 
@@ -473,27 +501,20 @@
     sequence = tokens * n
     width = stream.shape[2]
     heads = HEADS // n
-    per_group = HEADS // KV_HEADS
     me = lax.axis_index("ctx")
     clip_length = clip_lengths[0]
 
-    groups = [(c * heads) // per_group for c in range(n)]
-    pieces = jnp.stack(
-        [
-            jnp.concatenate(
-                [
-                    queries[0, :, c * heads * HEAD : (c + 1) * heads * HEAD],
-                    keys[0, :, groups[c] * HEAD : (groups[c] + 1) * HEAD],
-                    values[0, :, groups[c] * HEAD : (groups[c] + 1) * HEAD],
-                ],
-                axis=-1,
-            )
-            for c in range(n)
-        ]
-    )
     is_live = jnp.arange(sequence, dtype=jnp.int32) < clip_length
     swapped, weight, attended, log_total, product = front(
-        pieces, out_weight, is_live.astype(jnp.float32)[None], n, dp_n, heads, 0
+        queries[0],
+        keys[0],
+        values[0],
+        out_weight,
+        is_live.astype(jnp.float32)[None],
+        n,
+        dp_n,
+        heads,
+        0,
     )
     swapped = swapped.reshape(sequence, (heads + 2) * HEAD)
     query_heads = swapped[:, : heads * HEAD].reshape(sequence, heads, HEAD)
@@ -526,8 +547,16 @@
     )
     bundles = collect(bundle, n, 2).reshape(sequence, 3 * PATCH)
     gathered = bundles[:, :PATCH]
-    unit_full = collect(unit_rows.astype(jnp.bfloat16), n, 1).reshape(sequence, width)
-    unit_out = matmul("tc,rc->tr", unit_full, weight)
+    n_out = n // 2
+    unit_half = unit_rows.astype(jnp.bfloat16)
+    to_partner = [(c, c + 1 - 2 * (c % 2)) for c in range(n)]
+    held = [(me, unit_half)]
+    fars = []
+    for k in range(1, n_out):
+        moved = lax.ppermute(unit_half, "ctx", [(c, (c + 2 * k) % n) for c in range(n)])
+        fars.append((lax.rem(me + n - 2 * k, n), moved))
+    beside = lax.ppermute(unit_half, "ctx", to_partner)
+    swap_core = 1 - 2 * lax.rem(me, 2)
     gained_out = matmul("rc,cp->rp", weight, gained.astype(jnp.bfloat16)).astype(jnp.bfloat16)
     weight_sum = jnp.sum(weight.astype(jnp.float32), axis=-1)
 
@@ -556,7 +585,11 @@
     summed_slope = (
         head_slope - second_unit * jnp.mean(head_slope * second_unit, axis=-1, keepdims=True)
     ) / second_root
-    summed_slopes = collect(summed_slope.astype(jnp.bfloat16), n, 4).reshape(
+    slope_half, beside, moved = lax.optimization_barrier(
+        (summed_slope.astype(jnp.bfloat16), beside, [piece for _, piece in fars])
+    )
+    relays = [lax.ppermute(piece, "ctx", to_partner) for piece in moved]
+    summed_slopes = collect(slope_half, n, 4).reshape(
         row_total, reward_width
     )
     active_slope = matmul("rw,hw->rh", summed_slopes, down_weight)
@@ -572,6 +605,7 @@
         / own_rows(first_root)
     )
     token_slope = matmul("rw,pw->rp", embed_slope.astype(jnp.bfloat16), embed_weight)
+    token_slope, relays = lax.optimization_barrier((token_slope, relays))
     token_slopes = collect(
         jnp.concatenate([token_slope, jnp.broadcast_to(row_rewards, (rows, PATCH))], axis=-1), n, 6
     ).reshape(row_total, 2 * PATCH)
@@ -588,6 +622,15 @@
         - unit_rows * jnp.mean(modulated_slope * unit_rows, axis=-1, keepdims=True)
     ) * inverse
     grad_stream = residual_slope.astype(jnp.bfloat16)
+
+    held += [(me + swap_core, beside)]
+    for (owner, _), piece, relay in zip(fars, moved, relays):
+        held += [(owner, piece), (owner + swap_core, relay)]
+    unit_out = jnp.zeros((n, tokens, out_weight.shape[0]), jnp.float32)
+    for owner, piece in held:
+        part = matmul("tc,rc->tr", piece, weight)
+        unit_out = lax.dynamic_update_slice_in_dim(unit_out, part[None], owner, 0)
+    unit_out = unit_out.reshape(sequence, out_weight.shape[0])
 
     noise_wide = noise_slopes.astype(jnp.float32)
     slope_mean = jnp.sum(noise_wide * gained_mean, axis=-1, keepdims=True)

time: 206 us -> 249 us (1.21)
  local copies, waits for them, and re-layouts: 12.1 us -> 45 us
  matrix products: 36.2 us -> 49.2 us
  Pallas kernels: 141 us -> 129 us
  other arithmetic: 11.6 us -> 17.7 us
    dynamic_update_slice x0 -> x4, local copies, waits for them, and re-layouts: none -> 31.4 us  [per_device(): unit_out = lax.dynamic_update_slice_in_dim(unit_out, part[None], owner, 0)]
    dot_general x7 -> x10, matrix products: 26 us -> 38.5 us  [matmul(): jnp.einsum(subscripts, left, right, preferred_element_type=jnp.float32)]
    pallas_call x4 -> x3, Pallas kernels: 48.3 us -> 36.2 us  [collect(): pl.pallas_call(functools.partial(collect_kernel, n), out_shape=jax.ShapeD...]
    broadcast_in_dim x0 -> x1, other arithmetic: none -> 3.86 us  [per_device(): return (jnp.reshape(reward, (1,)), grad_stream[None], grad_queries[None])]
    unnamed x49 -> x45, local copies, waits for them, and re-layouts: 4.32 us -> 7.3 us
    squeeze x3 -> x0, local copies, waits for them, and re-layouts: 2.88 us -> none  [the longest x1 1.18 us: per_device(): queries[0, :, c * heads * HEAD:(c + 1) * heads * HEAD]]
  transfers between devices with their start and end apart: 0 -> 3, of which waited for: 0 -> 0; matrix products, arithmetic and copies ran while one was open for 0% -> 24% of each run, Pallas kernels for 0% -> 16%
where the time goes in v3:
time: 249 us; the launch traced here: 248 us
  Pallas kernels  129 us (52%)
  matrix products  49.2 us (20%)
  local copies, waits for them, and re-layouts  45 us (18%)
  other arithmetic  17.7 us (7%)
  between operations  4.46 us (2%)
    pallas_call x1, Pallas kernels, front(): pl.pallas_call(functools.partial(front_kernel, n, dp_n, heads), out_shape...  68.5 us
    dot_general x10, matrix products, matmul(): jnp.einsum(subscripts, left, right, preferred_element_type=jnp.float32)  38.5 us
    pallas_call x3, Pallas kernels, collect(): pl.pallas_call(functools.partial(collect_kernel, n), out_shape=jax.ShapeD...  36.2 us
    dynamic_update_slice x4, local copies, waits for them, and re-layouts, per_device(): unit_out = lax.dynamic_update_slice_in_dim(unit_out, part[None], owner, 0)  31.4 us
    pallas_call x2, Pallas kernels, reduce(): pl.pallas_call(functools.partial(reduce_kernel, n), out_shape=jax.ShapeDt...  16.3 us
    pallas_call x1, Pallas kernels, swap(): pl.pallas_call(functools.partial(swap_kernel, n), out_shape=jax.ShapeDtyp...  8.19 us
    unnamed x45, local copies, waits for them, and re-layouts  7.3 us
  transfers between devices with their start and end apart: 3, of which 0 were waited for; matrix products, arithmetic and copies ran while one was open for 24% of the time, Pallas kernels for 16%

profile of v3, /device:TPU:1, one launch (start us, length us, event | category | flops | bytes accessed | tf_op | source)
XLA Modules:
  0.0 247.6 jit_solution(17594393094309353596)
XLA Ops:
  5.2 68.5 %shard_map.193 = (bf16[4,128,768]{2,1,0:T(8,128)(2,1)S(1)}, bf16[512,4096]{1,0:T(8,128)(2,1)}, bf16[512,512]{1,0:T(8,128)(2,1)S(1)}, f32[512,4]{1,0:T(8,128)S(1)}, f32[128,4096]{1,0:T(8,128)S(1)}) custom-call(bf16[128,2048]{1,0:T(8,128)(2,1)S(1)} %bitcast.121, bf16[128,512]{1,0:T(8,128)(2,1)S(1)} %bitcast.123, bf16[128,512]{1,0:T(8,128)(2,1)S(1)} %bitcast.124, ...), custom_call_target="tpu_custom_call" | custom-call | bytes 24000000 | tf_op jit(solution)/shard_map/pallas_call | solution.py:309
  73.8 1.6 fusion.76
  75.8 1.3 fusion.16
  79.8 2.2 fusion.3
  81.9 2.3 fusion.52
  84.4 22.6 %shard_map.194 = bf16[4,128,384]{2,1,0:T(8,128)(2,1)S(1)} custom-call(bf16[128,384]{1,0:T(8,128)(2,1)S(1)} %pad_maximum_fusion.src), custom_call_target="tpu_custom_call" | custom-call | bytes 24000000 | tf_op jit(solution)/shard_map/pallas_call | solution.py:371
  107.1 2.5 %fusion.79 = f32[128,512]{0,1:T(8,128)S(1)} fusion(bf16[128,4096]{1,0:T(8,128)(2,1)} %fusion.16, bf16[512,4096]{1,0:T(8,128)(2,1)S(1)} %copy-done.5), kind=kOutput, calls=%fused_computation.137 | convolution fusion | flops 536870912 | bytes 5505024 | tf_op jit(solution)/shard_map/tc,rc->tr/dot_general | solution.py:475
  114.2 3.6 %fusion.42 = f32[256,1536]{1,0:T(8,128)S(1)} fusion(bf16[1408,1536]{1,0:T(8,128)(2,1)} %param.32, f32[256,1408]{1,0:T(8,128)S(1)} %broadcast_divide_fusion, f32[1408]{0:T(1024)S(1)} %copy-done.17), kind=kOutput, calls=%fused_computation.63 | convolution fusion | flops 1108017152 | bytes 7345664 | tf_op jit(solution)/shard_map/dot_general | solution.py:569
  117.8 4.3 %convolution_convert_fusion.1 = bf16[256,1408]{1,0:T(8,128)(2,1)S(1)} fusion(bf16[1536,1408]{1,0:T(8,128)(2,1)} %param.33, f32[256,1536]{1,0:T(8,128)S(1)} %fusion.42), kind=kOutput, calls=%fused_computation.12 | convolution fusion | flops 1111195648 | bytes 6619136 | tf_op jit(solution)/shard_map/dot_general | solution.py:578
  122.1 7.9 %shard_map.195 = f32[64,1408]{1,0:T(8,128)S(1)} custom-call(bf16[4,64,1408]{2,1,0:T(8,128)(2,1)S(1)} %bitcast.117), custom_call_target="tpu_custom_call" | custom-call | bytes 24000000 | tf_op jit(solution)/shard_map/pallas_call | solution.py:445
  133.3 1.3 reshape.194
  136.1 7.9 %dynamic_update_slice.12 = f32[4,128,512]{1,0,2:T(4,128)} dynamic-update-slice(f32[4,128,512]{1,0,2:T(4,128)} %broadcast_in_dim.42, f32[1,128,512]{1,0,2:T(1,128)S(1)} %bitcast.129, s32[]{:T(128)S(6)} %select_n.55, s32[]{:T(128)} %constant.34.clone.1, s32[]{:T(128)} %constant.34.clone.1) | dynamic-update-slice | bytes 524292 | tf_op jit(solution)/shard_map/dynamic_update_slice | solution.py:632
  143.9 2.7 %fusion.50 = f32[512,512,4]{1,0,2:T(8,128)} fusion(bf16[512,4,128]{0,2,1:T(8,128)(2,1)S(1)} %bitcast.125, bf16[512,768]{1,0:T(8,128)(2,1)S(1)} %bitcast.119), kind=kOutput, calls=%fused_computation.87 | convolution fusion | flops 268435456 | bytes 4849664 | tf_op jit(solution)/shard_map/thd,sd->hts/dot_general | solution.py:475
  146.7 8.0 %shard_map.196 = bf16[4,64,1408]{2,1,0:T(8,128)(2,1)S(1)} custom-call(bf16[64,1408]{1,0:T(8,128)(2,1)S(1)} %fusion.74.src), custom_call_target="tpu_custom_call" | custom-call | bytes 24000000 | tf_op jit(solution)/shard_map/pallas_call | solution.py:371
  154.7 7.0 %convolution_convert_fusion = bf16[256,1408]{1,0:T(8,128)(2,1)S(1)} fusion(bf16[1408,1536]{1,0:T(8,128)(2,1)} %param.32, f32[256,1536]{1,0:T(8,128)} %copy-done.21, bf16[256,1408]{1,0:T(8,128)(2,1)S(1)} %bitcast.116, bf16[1536,1408]{1,0:T(8,128)(2,1)} %param.33), kind=kOutput, calls=%fused_computation.11 | convolution fusion | flops 2222817280 | bytes 11665408 | tf_op jit(solution)/shard_map/rh,wh->rw/dot_general | solution.py:475
  162.0 3.8 %fusion.80 = f32[128,512]{0,1:T(8,128)S(1)} fusion(bf16[128,4096]{1,0:T(8,128)(2,1)} %collective-permute-done, bf16[512,4096]{1,0:T(8,128)(2,1)} %get-tuple-element.19), kind=kOutput, calls=%fused_computation.138 | convolution fusion | flops 536870912 | bytes 5505024 | tf_op jit(solution)/shard_map/tc,rc->tr/dot_general | solution.py:475
  165.8 8.3 %shard_map.197 = f32[64,1408]{1,0:T(8,128)S(1)} custom-call(bf16[4,64,1408]{2,1,0:T(8,128)(2,1)S(1)} %bitcast.115), custom_call_target="tpu_custom_call" | custom-call | bytes 24000000 | tf_op jit(solution)/shard_map/pallas_call | solution.py:445
  174.1 7.9 %dynamic_update_slice.13 = f32[4,128,512]{1,0,2:T(4,128)} dynamic-update-slice(f32[4,128,512]{1,0,2:T(4,128)} %dynamic_update_slice.12, f32[1,128,512]{1,0,2:T(1,128)S(1)} %bitcast.131, s32[]{:T(128)S(6)} %select_n.56, s32[]{:T(128)} %constant.34.clone.1, s32[]{:T(128)} %constant.34.clone.1) | dynamic-update-slice | bytes 524292 | tf_op jit(solution)/shard_map/dynamic_update_slice | solution.py:632
  182.0 4.6 %fusion.81 = f32[128,512]{0,1:T(8,128)} fusion(bf16[128,4096]{1,0:T(8,128)(2,1)} %collective-permute-done.1, bf16[512,4096]{1,0:T(8,128)(2,1)} %get-tuple-element.19), kind=kOutput, calls=%fused_computation.139 | convolution fusion | flops 536870912 | bytes 5505024 | tf_op jit(solution)/shard_map/tc,rc->tr/dot_general | solution.py:475
  186.5 7.9 %dynamic_update_slice.14 = f32[4,128,512]{1,0,2:T(4,128)} dynamic-update-slice(f32[4,128,512]{1,0,2:T(4,128)} %dynamic_update_slice.13, f32[1,128,512]{1,0,2:T(1,128)} %bitcast.132, s32[]{:T(128)S(6)} %select_n.57, s32[]{:T(128)} %constant.34.clone.1, s32[]{:T(128)} %constant.34.clone.1) | dynamic-update-slice | bytes 524292 | tf_op jit(solution)/shard_map/dynamic_update_slice | solution.py:632
  194.6 1.3 fusion.46
  195.9 5.6 %shard_map.198 = f32[4,64,256]{2,1,0:T(8,128)S(1)} custom-call(f32[64,256]{1,0:T(8,128)S(1)} %pad_maximum_fusion.1.src), custom_call_target="tpu_custom_call" | custom-call | bytes 24000000 | tf_op jit(solution)/shard_map/pallas_call | solution.py:371
  201.5 1.5 scatter_custom_fusion
  203.6 3.8 %fusion.82 = f32[128,512]{0,1:T(8,128)S(1)} fusion(bf16[128,4096]{1,0:T(8,128)(2,1)} %collective-permute-done.2, bf16[512,4096]{1,0:T(8,128)(2,1)} %get-tuple-element.19), kind=kOutput, calls=%fused_computation.140 | convolution fusion | flops 536870912 | bytes 5505024 | tf_op jit(solution)/shard_map/tc,rc->tr/dot_general | solution.py:475
  207.7 7.9 %dynamic_update_slice.15 = f32[4,128,512]{1,0,2:T(4,128)} dynamic-update-slice(f32[4,128,512]{1,0,2:T(4,128)} %dynamic_update_slice.14, f32[1,128,512]{1,0,2:T(1,128)S(1)} %bitcast.130, s32[]{:T(128)S(6)} %select_n.58, s32[]{:T(128)} %constant.34.clone.1, s32[]{:T(128)} %constant.34.clone.1) | dynamic-update-slice | bytes 524292 | tf_op jit(solution)/shard_map/dynamic_update_slice | solution.py:632
  215.6 5.0 %fusion.18 = bf16[512,512]{0,1:T(8,128)(2,1)} fusion(bf16[512,128]{1,0:T(8,128)(2,1)S(1)} %get-tuple-element.40, bf16[512,4096]{1,0:T(8,128)(2,1)} %get-tuple-element.19, bf16[4096,128]{1,0:T(8,128)(2,1)S(1)} %copy-done.9, f32[64,8,4,128]{3,2,1,0:T(4,128)} %bitcast.128, f32[4096]{0:T(1024)S(1)} %bitcast.137, f32[512]{0:T(512)S(1)} %convert_reduce_fusion.1, ...), kind=kOutput, calls=%fused_computation.40 | convolution fusion | flops 607191040 | bytes 6971392 | tf_op jit(solution)/shard_map/tp,rp->tr/dot_general | solution.py:475
  220.6 1.4 copy.65
  221.9 1.9 multiply_reduce_fusion.3
  223.9 4.3 %fusion.20 = bf16[512,4,128]{2,0,1:T(8,128)(2,1)S(1)} fusion(f32[512,512,4]{1,0,2:T(8,128)} %fusion.50, bf16[512,4,128]{0,2,1:T(8,128)(2,1)} %bitcast.134, f32[4,512]{1,0:T(4,128)S(1)} %copy.66, f32[4,512]{1,0:T(4,128)S(1)} %copy.59, pred[512]{0:T(512)(128)(4,1)S(1)} %copy-done.20, bf16[512,768]{1,0:T(8,128)(2,1)S(1)} %bitcast.120), kind=kOutput, calls=%fused_computation.42 | convolution fusion | flops 543686656 | bytes 5521920 | tf_op jit(solution)/shard_map/hts,sd->htd/dot_general | solution.py:475
  228.9 8.2 %shard_map.199 = bf16[4,128,512]{2,1,0:T(8,128)(2,1)S(1)} custom-call(bf16[4,128,512]{2,1,0:T(8,128)(2,1)S(1)} %convert_element_type.143.src), custom_call_target="tpu_custom_call" | custom-call | bytes 24000000 | tf_op jit(solution)/shard_map/pallas_call | solution.py:74
  238.4 3.5 %fusion.75 = (f32[128]{0:T(128)S(1)}, f32[128]{0:T(128)S(1)}, f32[128,4096]{1,0:T(8,128)}) fusion(f32[128]{0:T(128)S(1)} %get-tuple-element.46, f32[128,4096]{1,0:T(8,128)} %copy-done.6, f32[128]{0:T(128)S(1)} %broadcast_multiply_fusion.6, f32[4096]{0:T(1024)S(1)} %bitcast.138, bf16[4096,128]{1,0:T(8,128)(2,1)S(1)} %copy-done.9, ...), kind=kOutput, calls=%fused_computation.134 | convolution fusion | flops 137363200 | bytes 5294084 | tf_op jit(solution)/shard_map/tp,dp->td/dot_general | solution.py:475
  242.6 3.9 %fusion.22 = bf16[1,128,4096]{2,1,0:T(8,128)(2,1)} fusion(f32[128,4096]{1,0:T(8,128)} %copy-done.6, f32[128,4096]{1,0:T(8,128)} %get-tuple-element.50, f32[128]{0:T(128)S(1)} %get-tuple-element.51, f32[128]{0:T(128)S(1)} %get-tuple-element.52, f32[128]{0:T(128)S(1)} %get-tuple-element.46, f32[128]{0:T(128)S(1)} %broadcast_multiply_fusion.6), kind=kLoop, calls=%fused_computation.45 | loop fusion | flops 3670016 | bytes 5244928 | tf_op jit(solution)/shard_map/broadcast_in_dim | solution.py:669
  (93 shorter events, 18.9 us)
Async XLA Ops:
  0.6 110.6 %copy-start = (bf16[128,1408]{1,0:T(8,128)(2,1)S(1)}, bf16[128,1408]{1,0:T(8,128)(2,1)}, u32[]{:S(2)}) copy-start(bf16[128,1408]{1,0:T(8,128)(2,1)} %param.30) | copy-start | bytes 1081348
  1.4 1.0 copy-start.1
  2.4 1.0 copy-start.2
  3.4 0.9 copy-start.3
  4.3 0.9 copy-start.4
  75.4 1.7 copy-start.6
  75.7 3.2 %copy-start.16 = (f32[1,4096]{1,0:T(1,128)S(1)}, f32[1,4096]{1,0:T(1,128)}, u32[]{:S(2)}) copy-start(f32[1,4096]{1,0:T(1,128)} %param.24) | copy-start | bytes 49156
  75.7 4.0 %copy-start.8 = (bf16[4096,128]{1,0:T(8,128)(2,1)S(1)}, bf16[4096,128]{1,0:T(8,128)(2,1)}, u32[]{:S(2)}) copy-start(bf16[4096,128]{1,0:T(8,128)(2,1)} %param.26) | copy-start | bytes 3145732
  75.8 4.0 %copy-start.15 = (f32[1,4096]{1,0:T(1,128)S(1)}, f32[1,4096]{1,0:T(1,128)}, u32[]{:S(2)}) copy-start(f32[1,4096]{1,0:T(1,128)} %param.23) | copy-start | bytes 49156
  75.8 6.2 %copy-start.19 = (bf16[1,128,128]{2,1,0:T(8,128)(2,1)S(1)}, bf16[1,128,128]{2,1,0:T(8,128)(2,1)}, u32[]{:S(2)}) copy-start(bf16[1,128,128]{2,1,0:T(8,128)(2,1)} %param.27) | copy-start | bytes 98308
  77.1 69.6 %collective-permute-start = (bf16[128,4096]{1,0:T(8,128)(2,1)}, bf16[128,4096]{1,0:T(8,128)(2,1)}, u32[]{:S(2)}, u32[]{:S(2)}) collective-permute-start(bf16[128,4096]{1,0:T(8,128)(2,1)} %fusion.16), channel_id=1, source_target_pairs={{0,1},{1,0},{2,3},{3,2},{4,5},{5,4},{6,7},{7,6},{8,9},{9,8},{10,11... | collective-permute-start | bytes 3145736 | tf_op jit(solution)/shard_map/ppermute | solution.py:558
  78.2 68.5 %collective-permute-start.1 = (bf16[128,4096]{1,0:T(8,128)(2,1)}, bf16[128,4096]{1,0:T(8,128)(2,1)}, u32[]{:S(2)}, u32[]{:S(2)}) collective-permute-start(bf16[128,4096]{1,0:T(8,128)(2,1)} %fusion.16), channel_id=1, source_target_pairs={{0,2},{1,3},{2,0},{3,1},{4,6},{5,7},{6,4},{7,5},{8,10},{9,11},{10,... | collective-permute-start | bytes 3145736 | tf_op jit(solution)/shard_map/ppermute | solution.py:556
  81.9 25.2 %copy-start.5 = (bf16[512,4096]{1,0:T(8,128)(2,1)S(1)}, bf16[512,4096]{1,0:T(8,128)(2,1)}, u32[]{:S(2)}) copy-start(bf16[512,4096]{1,0:T(8,128)(2,1)} %get-tuple-element.19) | copy-start | bytes 12582916
  109.6 0.7 copy-start.18
  111.2 3.0 %copy-start.17 = (f32[1408]{0:T(1024)S(1)}, f32[1408]{0:T(1024)}, u32[]{:S(2)}) copy-start(f32[1408]{0:T(1024)} %param.31) | copy-start | bytes 16900
  111.7 1.1 copy-start.7
  113.0 1.2 copy-start.10
  117.8 4.3 %copy-start.21 = (f32[256,1536]{1,0:T(8,128)}, f32[256,1536]{1,0:T(8,128)S(1)}, u32[]{:S(2)}) copy-start(f32[256,1536]{1,0:T(8,128)S(1)} %fusion.42) | copy-start | bytes 4718596
  117.8 13.4 %copy-start.13 = (f32[1408]{0:T(1024)S(1)}, f32[1408]{0:T(1024)}, u32[]{:S(2)}) copy-start(f32[1408]{0:T(1024)} %param.34) | copy-start | bytes 16900
  117.8 13.4 %copy-start.14 = (f32[1408]{0:T(1024)S(1)}, f32[1408]{0:T(1024)}, u32[]{:S(2)}) copy-start(f32[1408]{0:T(1024)} %param.35) | copy-start | bytes 16900
  132.5 14.1 %copy-start.12 = (f32[64,1408]{1,0:T(8,128)}, f32[64,1408]{1,0:T(8,128)S(1)}, u32[]{:S(2)}) copy-start(f32[64,1408]{1,0:T(8,128)S(1)} %get-tuple-element.41) | copy-start | bytes 1081348
  161.8 34.0 %collective-permute-start.2 = (bf16[128,4096]{1,0:T(8,128)(2,1)}, bf16[128,4096]{1,0:T(8,128)(2,1)}, u32[]{:S(2)}, u32[]{:S(2)}) collective-permute-start(bf16[128,4096]{1,0:T(8,128)(2,1)} %collective-permute-done.1), channel_id=1, source_target_pairs={{0,1},{1,0},{2,3},{3,2},{4,5},{5,4},{6,7},{7,6},{8,9},{9,8},{10,11... | collective-permute-start | bytes 3145736 | tf_op jit(solution)/shard_map/ppermute | solution.py:591
  182.0 12.4 %copy-start.11 = (f32[256,1408]{1,0:T(8,128)S(1)}, f32[256,1408]{1,0:T(8,128)}, u32[]{:S(2)}) copy-start(f32[256,1408]{1,0:T(8,128)} %copy-done.10) | copy-start | bytes 4325380
  203.6 12.0 %copy-start.9 = (bf16[4096,128]{1,0:T(8,128)(2,1)S(1)}, bf16[4096,128]{1,0:T(8,128)(2,1)}, u32[]{:S(2)}) copy-start(bf16[4096,128]{1,0:T(8,128)(2,1)} %param.26) | copy-start | bytes 3145732
  220.6 3.3 %copy-start.20 = (pred[512]{0:T(512)(128)(4,1)S(1)}, pred[512]{0:T(512)(128)(4,1)}, u32[]{:S(2)}) copy-start(pred[512]{0:T(512)(128)(4,1)} %iota_compare_fusion) | copy-start | bytes 1540
